TPU v7x, 32 devices: a whole 2x2x4 slice. The times are simulated.
32 devices in a mesh: dp: 8 (over y, x, core), tensor: 4 (over z).
Axes of the slice: x: 2, y: 2, z: 4, core: 2. Of those that a mesh axis runs over, the one named last changes fastest.
Arguments:
- block_input: bfloat16 [1536, 1536], P('dp'), may hold values from -6 to 6
- segments: int32 [1536], P('dp'), may hold values from 0 to 2, as said below
- positions: int32 [1536], P('dp'), may hold values from 0 to 191, as said below
- cotangent: bfloat16 [1536, 1536], P('dp'), may hold values from -6 to 6
- gain_attn: float32 [1536], replicated, may hold values from 0.1 to 1.9
- w_query: bfloat16 [1536, 1536], P(None, 'tensor'), may hold values from -0.15625 to 0.15625
- b_query: float32 [1536], P('tensor'), may hold values from -3 to 3
- w_key: bfloat16 [1536, 256], replicated, may hold values from -0.15625 to 0.15625
- b_key: float32 [256], replicated, may hold values from -3 to 3
- w_value: bfloat16 [1536, 256], replicated, may hold values from -0.15625 to 0.15625
- b_value: float32 [256], replicated, may hold values from -3 to 3
- w_out: bfloat16 [1536, 1536], P('tensor'), may hold values from -0.4375 to 0.4375
- gain_mlp: float32 [1536], replicated, may hold values from 0.1 to 1.9
- w_gate: bfloat16 [1536, 8960], P(None, 'tensor'), may hold values from -0.15625 to 0.15625
- w_up: bfloat16 [1536, 8960], P(None, 'tensor'), may hold values from -0.15625 to 0.15625
- w_down: bfloat16 [8960, 1536], P('tensor'), may hold values from -0.0625 to 0.0625
Outputs:
- output: float32 [1536, 1536], P('dp')
- d_input: float32 [1536, 1536], P('dp')
- grad_gain_attn: float32 [1536], replicated
- grad_w_query: float32 [1536, 1536], P('dp', 'tensor')
- grad_b_query: float32 [1536], replicated
- grad_w_key: float32 [1536, 256], P(('dp', 'tensor'))
- grad_b_key: float32 [256], replicated
- grad_w_value: float32 [1536, 256], P(('dp', 'tensor'))
- grad_b_value: float32 [256], replicated
- grad_w_out: float32 [1536, 1536], P('tensor', 'dp')
- grad_gain_mlp: float32 [1536], replicated
- grad_w_gate: float32 [1536, 8960], P('dp', 'tensor')
- grad_w_up: float32 [1536, 8960], P('dp', 'tensor')
- grad_w_down: float32 [8960, 1536], P('tensor', 'dp')
Inputs may be any that keep to these rules, and one draw needn't show every extreme that they name: `segments`: within each packed sequence of 192 tokens the segment number starts at 0 and rises by one at each new document; each document holds 32 to 192 tokens. `positions`: each token's index within its document.
All inputs are finite; a program needn't handle non-finite values.
Results may differ from a plain program's by a relative error of at most 0.019.
The roundings to bfloat16 on the way count: a program that leaves them out, or rounds other values in their place, can miss the bound.
Values may be sent and summed in bfloat16 or wider, within the bound.
No kernel may reach another device: no remote copies, remote signals or barrier semaphores. Data moves between devices by JAX's collectives and lax.ppermute only.
A program may use at most 192 MiB of HBM per device.

v0:
```python
import functools
import math

import jax
import jax.numpy as jnp
from jax import lax
from jax.experimental import pallas as pl
from jax.experimental.pallas import tpu as pltpu
from jax.sharding import PartitionSpec as P


H = 12
KVH = 2
HD = 128
SEQ = 192


eps = 1e-06
theta = 1000000.0


def rope_tables(positions):
    exponent = jnp.arange(0, HD, 2).astype(jnp.float32) / HD
    frequency = jnp.power(jnp.float32(theta), -exponent)
    angles = positions.astype(jnp.float32)[:, None] * frequency[None, :]
    cosine = jnp.concatenate([jnp.cos(angles), jnp.cos(angles)], axis=1)
    sine_table = jnp.concatenate([jnp.sin(angles), jnp.sin(angles)], axis=1)
    return (cosine, sine_table)


def rotate(values):
    first_half = values[..., : HD // 2]
    second = values[..., HD // 2 :]
    return jnp.concatenate([-second, first_half], axis=-1)


def rope_apply(values, cosine, sine_table):
    return values * cosine[:, None, :] + rotate(values) * sine_table[:, None, :]


def rope_back(gradient, cosine, sine_table):
    return gradient * cosine[:, None, :] - rotate(gradient * sine_table[:, None, :])


def norm_back(values, rscale, gain, upstream):
    scaled = gain * upstream
    return rscale * (
        scaled - values * rscale * rscale * jnp.mean(scaled * values, axis=1, keepdims=True)
    )


def swap(values, axis, step):
    size = lax.axis_size(axis)
    return lax.ppermute(values, axis, [(rank, rank ^ step) for rank in range(size)])


def gather_dp(own):
    parts = lax.axis_size("dp")
    near, far = [own], []
    if parts == 8:
        half = own.shape[0] // 2
        along_x = swap(own, "dp", 2)
        along_y = swap(own, "dp", 4)
        near = [own, along_x, along_y]
        far = [swap(along_y[:half], "dp", 2), swap(along_x[half:], "dp", 4)]
    else:
        step = 2
        while step < parts:
            near = near + [swap(chip, "dp", step) for chip in near]
            step *= 2
    partner = [swap(chip, "dp", 1) for chip in near]
    partner += [swap(chip, "dp", 1) for chip in far]
    return near + far + partner


VMEM = pl.BlockSpec(memory_space=pltpu.VMEM)
SMEM = pl.BlockSpec(memory_space=pltpu.SMEM)
ANY = pl.BlockSpec(memory_space=pl.ANY)


def arrange_kernel(rank, *refs):
    blocks, out = refs[:-1], refs[-1]
    size = blocks[0].shape[0]
    for k, block in enumerate(blocks):
        start = pl.multiple_of((rank[0] ^ k) * size, size)
        out[pl.ds(start, size), :] = block[...].astype(out.dtype)


def arrange(own, axis, rank, dtype):
    parts = lax.axis_size(axis)
    blocks = [own] + [swap(own, axis, k) for k in range(1, parts)]
    size, width = own.shape
    return pl.pallas_call(
        arrange_kernel,
        out_shape=jax.ShapeDtypeStruct((parts * size, width), dtype),
        in_specs=[SMEM] + [VMEM] * parts,
        out_specs=VMEM,
        name="arrange",
    )(rank.reshape(1), *blocks)


def fetch(sources, target, sems, first):
    copies = []
    row = 0
    for k, source in enumerate(sources):
        rows = source.shape[0]
        copy = pltpu.make_async_copy(source, target.at[pl.ds(row, rows)], sems.at[first + k])
        copy.start()
        copies.append(copy)
        row += rows
    return copies


def product(a, b, dims):
    return lax.dot_general(a, b, (dims, ((), ())), preferred_element_type=jnp.float32)


def slice_kernel(count, parts, rank, *refs):
    normed_refs, cot_refs = refs[:count], refs[count : 2 * count]
    gate_up, down = refs[2 * count : 2 * count + 2]
    outs = refs[2 * count + 2 : 2 * count + 2 + parts]
    normed, cot, wide, narrow, pieces, sems = refs[2 * count + 2 + parts :]
    padded = down.shape[0]
    tokens, width = normed.shape
    _, units, rows = outs[0].shape
    f32, bf16 = jnp.float32, jnp.bfloat16
    waits = fetch(normed_refs, normed, sems, 0) + fetch(cot_refs, cot, sems, count)
    for copy in waits:
        copy.wait()
    chunk = 256

    def forward(step, carry):
        at = pl.ds(pl.multiple_of(step * chunk, chunk), chunk)
        pre = product(gate_up[...], normed[at, :], ((1,), (1,)))
        act = product(down[...], cot[at, :], ((1,), (1,))).astype(bf16).astype(f32)
        gate, up = pre[:padded], pre[padded:]
        sigmoid = jax.nn.sigmoid(gate)
        wide[:padded, at] = (act * up * sigmoid * (1.0 + gate * (1.0 - sigmoid))).astype(bf16)
        wide[padded:, at] = (act * gate * sigmoid).astype(bf16)
        narrow[:, at] = (gate * sigmoid * up).astype(bf16)
        return carry

    lax.fori_loop(0, tokens // chunk, forward, 0)
    block = 2 * rows if (2 * rows) % 128 == 0 else width
    per = block // rows

    def backward(step, carry):
        at = pl.ds(pl.multiple_of(step * block, block), block)
        both = product(wide[...], normed[:, at], ((1,), (0,))).astype(bf16)
        last = product(narrow[...], cot[:, at], ((1,), (0,))).astype(bf16)
        for k in range(per):
            cols = slice(k * rows, (k + 1) * rows)
            pieces[step * per + k, 0] = both[:units, cols]
            pieces[step * per + k, 1] = both[padded : padded + units, cols]
            pieces[step * per + k, 2] = last[:units, cols]
        return carry

    lax.fori_loop(0, width // block, backward, 0)
    for k in range(parts):
        outs[k][...] = pieces[rank[0] ^ k]


def slice_grads(normed_blocks, cot_blocks, gate_up, down, rank, parts, units):
    count = len(normed_blocks)
    padded, width = down.shape
    tokens = sum(block.shape[0] for block in normed_blocks)
    rows = width // parts
    bf16 = jnp.bfloat16
    return pl.pallas_call(
        functools.partial(slice_kernel, count, parts),
        out_shape=[jax.ShapeDtypeStruct((3, units, rows), bf16)] * parts,
        in_specs=[SMEM] + [ANY] * (2 * count) + [VMEM, VMEM],
        out_specs=[VMEM] * parts,
        scratch_shapes=[
            pltpu.VMEM((tokens, width), bf16),
            pltpu.VMEM((tokens, width), bf16),
            pltpu.VMEM((2 * padded, tokens), bf16),
            pltpu.VMEM((padded, tokens), bf16),
            pltpu.VMEM((parts, 3, units, rows), bf16),
            pltpu.SemaphoreType.DMA((2 * count,)),
        ],
        name="slice_grads",
    )(rank.reshape(1), *normed_blocks, *cot_blocks, gate_up, down)


def place_kernel(rank, *refs):
    parts = len(refs) - 4
    pieces, (gate_out, up_out, down_out, buffer) = refs[:parts], refs[parts:]
    units = pieces[0].shape[1]
    for k in range(parts):
        buffer[rank[0] ^ k] = pieces[k][...]
    for j in range(parts):
        gate_out[:, j * units : (j + 1) * units] = buffer[j, 0].astype(jnp.float32).T
        up_out[:, j * units : (j + 1) * units] = buffer[j, 1].astype(jnp.float32).T
        down_out[j * units : (j + 1) * units, :] = buffer[j, 2].astype(jnp.float32)


def place(pieces, rank):
    parts = len(pieces)
    _, units, rows = pieces[0].shape
    wide = jax.ShapeDtypeStruct((rows, parts * units), jnp.float32)
    tall = jax.ShapeDtypeStruct((parts * units, rows), jnp.float32)
    return pl.pallas_call(
        place_kernel,
        out_shape=(wide, wide, tall),
        in_specs=[SMEM] + [VMEM] * parts,
        out_specs=(VMEM, VMEM, VMEM),
        scratch_shapes=[pltpu.VMEM((parts,) + pieces[0].shape, jnp.bfloat16)],
        name="place",
    )(rank.reshape(1), *pieces)


def outer_kernel(left_count, right_count, *refs):
    left_refs = refs[:left_count]
    right_refs = refs[left_count : left_count + right_count]
    out, left, right, sems = refs[left_count + right_count :]
    waits = fetch(left_refs, left, sems, 0) + fetch(right_refs, right, sems, left_count)
    for copy in waits:
        copy.wait()
    out[...] = product(left[...], right[...], ((0,), (0,)))


def outer(left_blocks, right_blocks):
    tokens = sum(block.shape[0] for block in left_blocks)
    left_width, right_width = left_blocks[0].shape[1], right_blocks[0].shape[1]
    counts = (len(left_blocks), len(right_blocks))
    return pl.pallas_call(
        functools.partial(outer_kernel, *counts),
        out_shape=jax.ShapeDtypeStruct((left_width, right_width), jnp.float32),
        in_specs=[ANY] * sum(counts),
        out_specs=VMEM,
        scratch_shapes=[
            pltpu.VMEM((tokens, left_width), jnp.bfloat16),
            pltpu.VMEM((tokens, right_width), jnp.bfloat16),
            pltpu.SemaphoreType.DMA((sum(counts),)),
        ],
        name="outer",
    )(*left_blocks, *right_blocks)


def local(
    block_input,
    segments,
    positions,
    cotangent,
    gain_attn,
    w_query,
    b_query,
    w_key,
    b_key,
    w_value,
    b_value,
    w_out,
    gain_mlp,
    w_gate,
    w_up,
    w_down,
):
    bf16 = jnp.bfloat16
    f32 = jnp.float32
    dp = lax.axis_size("dp")
    tp = lax.axis_size("tensor")
    dp_rank = lax.axis_index("dp")
    tp_rank = lax.axis_index("tensor")
    row_count = block_input.shape[0]
    own_rows = row_count // tp
    width = block_input.shape[1]
    local_heads = w_query.shape[1] // HD
    score_scale = 1.0 / math.sqrt(HD)
    head_start = tp_rank * local_heads // (H // KVH) * HD
    slice_rows = width // dp

    def exchange_columns(values):
        blocks = []
        for k in [*range(0, dp, 2), *range(1, dp, 2)]:
            block = lax.dynamic_slice_in_dim(values, (dp_rank ^ k) * slice_rows, slice_rows, 1)
            blocks.append(swap(block, "dp", k) if k else block)
        return blocks

    def dot(a, b):
        return jnp.dot(a, b, preferred_element_type=f32)

    def own_block(values):
        return lax.dynamic_slice_in_dim(values, tp_rank * own_rows, own_rows, 0)

    def reduce_tensor(partial):
        sent = partial.astype(bf16)
        total = own_block(partial)
        for k in range(1, tp):
            block = lax.dynamic_slice_in_dim(sent, (tp_rank ^ k) * own_rows, own_rows, 0)
            total = total + swap(block, "tensor", k).astype(f32)
        return total

    cot = cotangent
    cot_blocks = gather_dp(cot)

    key_own = lax.dynamic_slice_in_dim(w_key, head_start, HD, 1)
    value_own = lax.dynamic_slice_in_dim(w_value, head_start, HD, 1)
    key_bias = lax.dynamic_slice_in_dim(b_key, head_start, HD, 0)
    value_bias = lax.dynamic_slice_in_dim(b_value, head_start, HD, 0)
    input_float = block_input.astype(f32)
    rscale_attn = lax.rsqrt(jnp.mean(input_float * input_float, axis=1, keepdims=True) + eps)
    normed_attn = (input_float * rscale_attn * gain_attn).astype(bf16)
    queries = dot(normed_attn, w_query) + b_query
    keys_pre = dot(normed_attn, key_own) + key_bias
    values_pre = dot(normed_attn, value_own) + value_bias
    cosine, sine_table = rope_tables(positions)
    query_rot = rope_apply(queries.reshape(row_count, local_heads, HD), cosine, sine_table).astype(bf16)
    key_rot = rope_apply(keys_pre.reshape(row_count, 1, HD), cosine, sine_table)[:, 0].astype(bf16)
    value_heads = values_pre.astype(bf16)
    order = jnp.arange(row_count)
    allowed = (
        (segments[:, None] == segments[None, :])
        & (order[None, :] <= order[:, None])
        & (order[None, :] // SEQ == order[:, None] // SEQ)
    )
    scores = jnp.einsum("thd,ud->htu", query_rot, key_rot, preferred_element_type=f32) * score_scale
    masked = jnp.where(allowed[None], scores, -1e30)
    row_top = jnp.max(masked, axis=2, keepdims=True)
    log_total = row_top + jnp.log(jnp.sum(jnp.exp(masked - row_top), axis=2, keepdims=True))
    probabilities = jnp.exp(masked - log_total)
    rounded_probs = probabilities.astype(bf16)
    heads_out = jnp.einsum("htu,ud->thd", rounded_probs, value_heads, preferred_element_type=f32).astype(bf16)
    heads_flat = heads_out.reshape(row_count, local_heads * HD)
    attention = dot(heads_flat, w_out)
    attention = reduce_tensor(attention)
    heads_blocks = gather_dp(heads_flat)
    normed_slice = exchange_columns(normed_attn)

    d_act = lax.dot_general(cot, w_down, (((1,), (1,)), ((), ())), preferred_element_type=f32)
    d_act = lax.optimization_barrier(d_act.astype(bf16))

    units = w_gate.shape[1] // dp
    padding = ((0, -units % 16), (0, 0))
    gate_slice = lax.dynamic_slice_in_dim(w_gate, dp_rank * units, units, 1).T
    up_slice = lax.dynamic_slice_in_dim(w_up, dp_rank * units, units, 1).T
    down_slice = lax.dynamic_slice_in_dim(w_down, dp_rank * units, units, 0)
    gate_up = jnp.concatenate([jnp.pad(gate_slice, padding), jnp.pad(up_slice, padding)])
    down_slice = jnp.pad(down_slice, padding)

    input_own = own_block(input_float)
    rscale_own = own_block(rscale_attn)
    hidden = input_own + attention
    rscale_mlp = lax.rsqrt(jnp.mean(hidden * hidden, axis=1, keepdims=True) + eps)
    normed_own = (hidden * rscale_mlp * gain_mlp).astype(bf16)
    normed_mlp = arrange(normed_own, "tensor", tp_rank, bf16)
    normed_blocks = gather_dp(normed_mlp)

    gate_pre = dot(normed_mlp, w_gate)
    up_pre = dot(normed_mlp, w_up)
    act_float = d_act.astype(f32)
    sigmoid_gate = jax.nn.sigmoid(gate_pre)
    activated = (gate_pre * sigmoid_gate * up_pre).astype(bf16)
    d_gate = (act_float * up_pre * sigmoid_gate * (1.0 + gate_pre * (1.0 - sigmoid_gate))).astype(bf16)
    d_up = (act_float * gate_pre * sigmoid_gate).astype(bf16)
    mlp_partial_grad = dot(d_gate, w_gate.T) + dot(d_up, w_up.T)
    d_normed_mlp = reduce_tensor(mlp_partial_grad)
    out_partial = lax.optimization_barrier(dot(activated, w_down))
    grad_gain_mlp = jnp.sum(d_normed_mlp * hidden * rscale_mlp, axis=0)
    d_hidden = own_block(cot).astype(f32) + norm_back(hidden, rscale_mlp, gain_mlp, d_normed_mlp)
    d_hidden_own = d_hidden.astype(bf16)
    d_hidden_b = arrange(d_hidden_own, "tensor", tp_rank, bf16)
    output_own = hidden + reduce_tensor(out_partial)
    output = arrange(output_own.astype(bf16), "tensor", tp_rank, f32)

    pieces = slice_grads(normed_blocks, cot_blocks, gate_up, down_slice, dp_rank, dp, units)
    pieces = [swap(piece, "dp", k) if k else piece for k, piece in enumerate(pieces)]
    summed_gate, summed_up, summed_down = place(pieces, dp_rank)
    d_hidden_slices = exchange_columns(d_hidden_b)
    summed_out = outer(heads_blocks, d_hidden_slices)

    d_heads = dot(d_hidden_b, w_out.T).astype(bf16).reshape(row_count, local_heads, HD)
    d_probs = jnp.einsum("thd,ud->htu", d_heads, value_heads, preferred_element_type=f32)
    delta = jnp.sum(d_heads.astype(f32) * heads_out.astype(f32), axis=2)
    d_scores = (probabilities * (d_probs - delta.T[:, :, None]) * score_scale).astype(bf16)
    d_qrot = jnp.einsum("htu,ud->thd", d_scores, key_rot, preferred_element_type=f32)
    d_krot = jnp.einsum("htu,thd->uhd", d_scores, query_rot, preferred_element_type=f32)
    d_vhead = jnp.einsum("htu,thd->uhd", rounded_probs, d_heads, preferred_element_type=f32)
    d_query = rope_back(d_qrot, cosine, sine_table)
    d_key = rope_back(d_krot, cosine, sine_table)
    query_grad = d_query.astype(bf16).reshape(row_count, local_heads * HD)
    key_grad = jnp.sum(d_key.astype(bf16).astype(f32), axis=1).astype(bf16)
    value_grad = jnp.sum(d_vhead.astype(bf16).astype(f32), axis=1).astype(bf16)
    attn_partial_grad = dot(query_grad, w_query.T) + dot(key_grad, key_own.T) + dot(value_grad, value_own.T)
    d_normed_attn = reduce_tensor(attn_partial_grad)
    factor_blocks = gather_dp(jnp.concatenate([query_grad, key_grad, value_grad], axis=1))
    grad_gain_attn = jnp.sum(d_normed_attn * input_own * rscale_own, axis=0)
    d_input_own = d_hidden + norm_back(input_own, rscale_own, gain_attn, d_normed_attn)
    d_input = arrange(d_input_own.astype(bf16), "tensor", tp_rank, f32)

    products = outer(normed_slice, factor_blocks)
    summed_query = products[:, : local_heads * HD]
    kv_products = products[:, local_heads * HD :]
    kv_rows = slice_rows // tp
    kv_total = [jnp.zeros((kv_rows, 2 * HD), f32) for _ in range(KVH)]
    for k in range(tp):
        block = lax.dynamic_slice_in_dim(kv_products, (tp_rank ^ k) * kv_rows, kv_rows, 0)
        block = swap(block, "tensor", k) if k else block
        source_head = (tp_rank ^ k) * local_heads // (H // KVH)
        for head in range(KVH):
            kv_total[head] = kv_total[head] + jnp.where(source_head == head, block, 0.0)
    summed_key = jnp.concatenate([total[:, :HD] for total in kv_total], axis=1)
    summed_value = jnp.concatenate([total[:, HD:] for total in kv_total], axis=1)

    bias_query = lax.dynamic_update_slice(
        jnp.zeros((H * HD,), f32),
        jnp.sum(d_query, axis=0).reshape(local_heads * HD),
        (tp_rank * local_heads * HD,),
    )
    bias_key = lax.dynamic_update_slice(
        jnp.zeros((KVH * HD,), f32), jnp.sum(d_key, axis=(0, 1)), (head_start,)
    )
    bias_value = lax.dynamic_update_slice(
        jnp.zeros((KVH * HD,), f32), jnp.sum(d_vhead, axis=(0, 1)), (head_start,)
    )
    small = jnp.concatenate([grad_gain_attn, grad_gain_mlp, bias_query, bias_key, bias_value]).reshape(-1, HD)
    for axis, size in (("dp", dp), ("tensor", tp)):
        step = 1
        while step < size:
            small = small + swap(small, axis, step)
            step *= 2
    small = small.reshape(-1)
    ends = [0, width, 2 * width, 2 * width + H * HD, 2 * width + (H + KVH) * HD, 2 * width + (H + 2 * KVH) * HD]
    gain_attn_sum, gain_mlp_sum, bias_query_sum, bias_key_sum, bias_value_sum = (
        small[a:b] for a, b in zip(ends[:-1], ends[1:])
    )
    return (
        output,
        d_input,
        gain_attn_sum,
        summed_query,
        bias_query_sum,
        summed_key,
        bias_key_sum,
        summed_value,
        bias_value_sum,
        summed_out,
        gain_mlp_sum,
        summed_gate,
        summed_up,
        summed_down,
    )


def solution(mesh):
    return jax.shard_map(
        local,
        mesh=mesh,
        in_specs=(
            P("dp", None),
            P("dp"),
            P("dp"),
            P("dp", None),
            P(),
            P(None, "tensor"),
            P("tensor"),
            P(),
            P(),
            P(),
            P(),
            P("tensor", None),
            P(),
            P(None, "tensor"),
            P(None, "tensor"),
            P("tensor", None),
        ),
        out_specs=(
            P("dp", None),
            P("dp", None),
            P(),
            P("dp", "tensor"),
            P(),
            P(("dp", "tensor"), None),
            P(),
            P(("dp", "tensor"), None),
            P(),
            P("tensor", "dp"),
            P(),
            P("dp", "tensor"),
            P("dp", "tensor"),
            P("tensor", "dp"),
        ),
        check_vma=False,
    )
```

profile of v0, /device:TPU:0, one launch (start us, length us, event | category | flops | bytes accessed | tf_op | source)
XLA Modules:
  0.0 343.2 jit_solution(11545322702987530136)
XLA Ops:
  12.6 5.1 %collective-permute-start.2 = (bf16[48,1536]{1,0:T(8,128)(2,1)}, bf16[48,1536]{1,0:T(8,128)(2,1)S(1)}, u32[]{:S(2)}, u32[]{:S(2)}) collective-permute-start(bf16[48,1536]{1,0:T(8,128)(2,1)} %get-tuple-element.102), channel_id=1, source_target_pairs={{0,3},{1,2},{2,1},{3,0},{4,7},{5,6},{6,5},{7,4},{8,11},{9,10},{10,... | collective-permute-start | bytes 442376 | tf_op jit(solution)/shard_map/ppermute | solution.py:54
  23.3 7.1 %collective-permute-done.1 = bf16[48,1536]{1,0:T(8,128)(2,1)} collective-permute-done((bf16[48,1536]{1,0:T(8,128)(2,1)}, bf16[48,1536]{1,0:T(8,128)(2,1)}, u32[]{:S(2)}, u32[]{:S(2)}) %collective-permute-start.1) | collective-permute-done | bytes 147488 | tf_op jit(solution)/shard_map/ppermute | solution.py:54
  32.1 3.1 collective-permute-start.4
  36.5 6.4 %convolution_convert_fusion = bf16[192,2240]{1,0:T(8,128)(2,1)} fusion(bf16[192,1536]{1,0:T(8,128)(2,1)} %refs_10_.1, bf16[2240,1536]{1,0:T(8,128)(2,1)} %param.31), kind=kOutput, calls=%fused_computation | convolution fusion | flops 1321635840 | bytes 8331264 | tf_op jit(solution)/shard_map/dot_general | solution.py:330
  52.0 5.6 %fusion.71 = f32[192,2240]{1,0:T(8,128)S(1)} fusion(bf16[192,1536]{1,0:T(8,128)(2,1)} %arrange.4.refs_0_, bf16[1536,2240]{0,1:T(8,128)(2,1)} %param.30), kind=kOutput, calls=%fused_computation.187 | convolution fusion | flops 1321205760 | bytes 9191424 | tf_op jit(solution)/shard_map/dot_general | solution.py:281
  57.6 5.4 %fusion.70 = f32[192,2240]{1,0:T(8,128)S(1)} fusion(bf16[192,1536]{1,0:T(8,128)(2,1)S(1)} %copy-done.1, bf16[1536,2240]{0,1:T(8,128)(2,1)} %param.29), kind=kOutput, calls=%fused_computation.186 | convolution fusion | flops 1321205760 | bytes 9191424 | tf_op jit(solution)/shard_map/dot_general | solution.py:281
  66.6 2.6 collective-permute-start.14
  72.8 2.6 collective-permute-done.14
  75.4 5.5 %collective-permute-done.13 = bf16[48,1536]{1,0:T(8,128)(2,1)S(1)} collective-permute-done((bf16[48,1536]{1,0:T(8,128)(2,1)S(1)}, bf16[48,1536]{1,0:T(8,128)(2,1)S(1)}, u32[]{:S(2)}, u32[]{:S(2)}) %collective-permute-start.13) | collective-permute-done | bytes 147488 | tf_op jit(solution)/shard_map/ppermute | solution.py:54
  88.0 2.9 collective-permute-done.15.refs_1_
  90.9 6.5 %collective-permute-done.16.refs_2_ = bf16[48,1536]{1,0:T(8,128)(2,1)S(1)} collective-permute-done((bf16[48,1536]{1,0:T(8,128)(2,1)S(1)}, bf16[48,1536]{1,0:T(8,128)(2,1)S(1)}, u32[]{:S(2)}, u32[]{:S(2)}) %collective-permute-start.16) | collective-permute-done | bytes 147488 | tf_op jit(solution)/shard_map/ppermute | solution.py:54
  119.4 4.2 %collective-permute-done.19 = bf16[48,1536]{1,0:T(8,128)(2,1)} collective-permute-done((bf16[48,1536]{1,0:T(8,128)(2,1)}, bf16[48,1536]{1,0:T(8,128)(2,1)}, u32[]{:S(2)}, u32[]{:S(2)}) %collective-permute-start.19) | collective-permute-done | bytes 147488 | tf_op jit(solution)/shard_map/ppermute | solution.py:54
  143.7 3.0 collective-permute-start.8
  152.4 4.5 %collective-permute-done.25 = f32[40,128]{1,0:T(8,128)S(1)} collective-permute-done((f32[40,128]{1,0:T(8,128)S(1)}, f32[40,128]{1,0:T(8,128)S(1)}, u32[]{:S(2)}, u32[]{:S(2)}) %collective-permute-start.25) | collective-permute-done | bytes 20512 | tf_op jit(solution)/shard_map/ppermute | solution.py:54
  157.1 3.8 %collective-permute-done.7 = bf16[48,1536]{1,0:T(8,128)(2,1)S(1)} collective-permute-done((bf16[48,1536]{1,0:T(8,128)(2,1)S(1)}, bf16[48,1536]{1,0:T(8,128)(2,1)S(1)}, u32[]{:S(2)}, u32[]{:S(2)}) %collective-permute-start.7) | collective-permute-done | bytes 147488 | tf_op jit(solution)/shard_map/ppermute | solution.py:54
  180.1 13.1 %collective-permute-done.36.refs_9_ = bf16[192,640]{1,0:T(8,128)(2,1)S(1)} collective-permute-done((bf16[192,640]{1,0:T(8,128)(2,1)S(1)}, bf16[192,640]{1,0:T(8,128)(2,1)S(1)}, u32[]{:S(2)}, u32[]{:S(2)}) %collective-permute-start.36) | collective-permute-done | bytes 245792 | tf_op jit(solution)/shard_map/ppermute | solution.py:54
  195.4 2.8 collective-permute-start.28
  198.2 4.7 %collective-permute-done.28 = f32[40,128]{1,0:T(8,128)} collective-permute-done((f32[40,128]{1,0:T(8,128)S(1)}, f32[40,128]{1,0:T(8,128)}, u32[]{:S(2)}, u32[]{:S(2)}) %collective-permute-start.28) | collective-permute-done | bytes 20512 | tf_op jit(solution)/shard_map/ppermute | solution.py:54
  204.6 7.0 %collective-permute-done.11.refs_3_ = bf16[48,1536]{1,0:T(8,128)(2,1)S(1)} collective-permute-done((bf16[48,1536]{1,0:T(8,128)(2,1)S(1)}, bf16[48,1536]{1,0:T(8,128)(2,1)S(1)}, u32[]{:S(2)}, u32[]{:S(2)}) %collective-permute-start.11) | collective-permute-done | bytes 147488 | tf_op jit(solution)/shard_map/ppermute | solution.py:54
  214.3 2.8 collective-permute-start.23
  218.6 5.2 %collective-permute-done.22.refs_2_ = bf16[48,1536]{1,0:T(8,128)(2,1)S(1)} collective-permute-done((bf16[48,1536]{1,0:T(8,128)(2,1)S(1)}, bf16[48,1536]{1,0:T(8,128)(2,1)S(1)}, u32[]{:S(2)}, u32[]{:S(2)}) %collective-permute-start.22) | collective-permute-done | bytes 147488 | tf_op jit(solution)/shard_map/ppermute | solution.py:54
  228.6 6.3 %collective-permute-done.38.refs_11_ = bf16[96,640]{1,0:T(8,128)(2,1)} collective-permute-done((bf16[96,640]{1,0:T(8,128)(2,1)S(1)}, bf16[96,640]{1,0:T(8,128)(2,1)}, u32[]{:S(2)}, u32[]{:S(2)}) %collective-permute-start.38) | collective-permute-done | bytes 122912 | tf_op jit(solution)/shard_map/ppermute | solution.py:54
  237.0 2.8 collective-permute-start.67
  249.6 3.0 outer.3
  256.4 3.4 outer.2
  264.1 2.4 collective-permute-start.45
  273.0 19.8 %slice_grads.1 = (bf16[3,280,192]{2,1,0:T(8,128)(2,1)}, bf16[3,280,192]{2,1,0:T(8,128)(2,1)}, bf16[3,280,192]{2,1,0:T(8,128)(2,1)}, bf16[3,280,192]{2,1,0:T(8,12...) custom-call(s32[1]{0:T(128)} %bitcast.20.rank, ...), custom_call_target="tpu_custom_call" | custom-call | tf_op jit(solution)/shard_map/slice_grads/pallas_call | solution.py:169
  298.5 7.4 %collective-permute-done.83.refs_2_ = bf16[3,280,192]{2,1,0:T(8,128)(2,1)S(1)} collective-permute-done((bf16[3,280,192]{2,1,0:T(8,128)(2,1)}, bf16[3,280,192]{2,1,0:T(8,128)(2,1)S(1)}, u32[]{:S(2)}, u32[]{:S(2)}) %collective-permute-start.83) | collective-permute-done | bytes 322592 | tf_op jit(solution)/shard_map/ppermute | solution.py:54
  307.7 6.3 %collective-permute-done.84.refs_3_ = bf16[3,280,192]{2,1,0:T(8,128)(2,1)S(1)} collective-permute-done((bf16[3,280,192]{2,1,0:T(8,128)(2,1)}, bf16[3,280,192]{2,1,0:T(8,128)(2,1)S(1)}, u32[]{:S(2)}, u32[]{:S(2)}) %collective-permute-start.84) | collective-permute-done | bytes 322592 | tf_op jit(solution)/shard_map/ppermute | solution.py:54
  314.1 20.2 %collective-permute-done.86.refs_5_ = bf16[3,280,192]{2,1,0:T(8,128)(2,1)} collective-permute-done((bf16[3,280,192]{2,1,0:T(8,128)(2,1)}, bf16[3,280,192]{2,1,0:T(8,128)(2,1)}, u32[]{:S(2)}, u32[]{:S(2)}) %collective-permute-start.86) | collective-permute-done | bytes 322592 | tf_op jit(solution)/shard_map/ppermute | solution.py:54
  334.3 6.1 %place.1 = (f32[192,2240]{1,0:T(8,128)}, f32[192,2240]{1,0:T(8,128)}, f32[2240,192]{1,0:T(8,128)}) custom-call(s32[1]{0:T(128)} %bitcast.20.rank, bf16[3,280,192]{2,1,0:T(8,128)(2,1)} %get-tuple-element.25.refs_0_, bf16[3,280,192]{2,1,0:T(8,128)(2,1)} %copy-done.44, bf16[3,280,192]{2,1,0:T(8,128)(2,1)} %copy-done.45, bf16[3,280,192]{2,1,0:T(8,128)(2,1)} %copy-done.46, ...), custom_call_target="tpu_custom_call" | custom-call | tf_op jit(solution)/shard_map/place/pallas_call | solution.py:203
  340.3 2.9 copy.56
  (483 shorter events, 156.5 us)
Async XLA Ops:
  18.9 27.3 %collective-permute-start.48 = (bf16[192,384]{1,0:T(8,128)(2,1)}, bf16[192,384]{1,0:T(8,128)(2,1)}, u32[]{:S(2)}, u32[]{:S(2)}) collective-permute-start(bf16[192,384]{1,0:T(8,128)(2,1)} %copy_bitcast_fusion.2.refs_0_), channel_id=1, source_target_pairs={{0,8},{4,12},{8,0},{12,4},{16,24},{20,28},{24,16},{28,20},{1,9},{5... | collective-permute-start | bytes 442376 | tf_op jit(solution)/shard_map/ppermute | solution.py:54
  20.6 24.1 %collective-permute-start.49 = (bf16[192,384]{1,0:T(8,128)(2,1)}, bf16[192,384]{1,0:T(8,128)(2,1)}, u32[]{:S(2)}, u32[]{:S(2)}) collective-permute-start(bf16[192,384]{1,0:T(8,128)(2,1)} %copy_bitcast_fusion.2.refs_0_), channel_id=1, source_target_pairs={{0,16},{4,20},{8,24},{12,28},{16,0},{20,4},{24,8},{28,12},{1,17},{... | collective-permute-start | bytes 442376 | tf_op jit(solution)/shard_map/ppermute | solution.py:54
  32.0 17.2 %collective-permute-start.3 = (bf16[48,1536]{1,0:T(8,128)(2,1)S(1)}, bf16[48,1536]{1,0:T(8,128)(2,1)S(1)}, u32[]{:S(2)}, u32[]{:S(2)}) collective-permute-start(bf16[48,1536]{1,0:T(8,128)(2,1)S(1)} %multiply_convert_fusion.3.refs_0_), channel_id=1, source_target_pairs={{0,1},{1,0},{2,3},{3,2},{4,5},{5,4},{6,7},{7,6},{8,9},{9,8},{10,11... | collective-permute-start | bytes 442376 | tf_op jit(solution)/shard_map/ppermute | solution.py:54
  32.1 17.1 %collective-permute-start.4 = (bf16[48,1536]{1,0:T(8,128)(2,1)S(1)}, bf16[48,1536]{1,0:T(8,128)(2,1)S(1)}, u32[]{:S(2)}, u32[]{:S(2)}) collective-permute-start(bf16[48,1536]{1,0:T(8,128)(2,1)S(1)} %multiply_convert_fusion.3.refs_0_), channel_id=1, source_target_pairs={{0,2},{1,3},{2,0},{3,1},{4,6},{5,7},{6,4},{7,5},{8,10},{9,11},{10,... | collective-permute-start | bytes 442376 | tf_op jit(solution)/shard_map/ppermute | solution.py:54
  35.2 14.1 %collective-permute-start.5 = (bf16[48,1536]{1,0:T(8,128)(2,1)S(1)}, bf16[48,1536]{1,0:T(8,128)(2,1)S(1)}, u32[]{:S(2)}, u32[]{:S(2)}) collective-permute-start(bf16[48,1536]{1,0:T(8,128)(2,1)S(1)} %multiply_convert_fusion.3.refs_0_), channel_id=1, source_target_pairs={{0,3},{1,2},{2,1},{3,0},{4,7},{5,6},{6,5},{7,4},{8,11},{9,10},{10,... | collective-permute-start | bytes 442376 | tf_op jit(solution)/shard_map/ppermute | solution.py:54
  44.7 96.7 %collective-permute-start.52 = (bf16[192,384]{1,0:T(8,128)(2,1)}, bf16[192,384]{1,0:T(8,128)(2,1)}, u32[]{:S(2)}, u32[]{:S(2)}) collective-permute-start(bf16[192,384]{1,0:T(8,128)(2,1)} %copy_bitcast_fusion.2.refs_0_), channel_id=1, source_target_pairs={{0,4},{4,0},{8,12},{12,8},{16,20},{20,16},{24,28},{28,24},{1,5},{5... | collective-permute-start | bytes 442376 | tf_op jit(solution)/shard_map/ppermute | solution.py:54
  46.2 84.2 %collective-permute-start.29 = (bf16[192,192]{1,0:T(8,128)(2,1)}, bf16[192,192]{1,0:T(8,128)(2,1)}, u32[]{:S(2)}, u32[]{:S(2)}) collective-permute-start(bf16[192,192]{1,0:T(8,128)(2,1)} %get-tuple-element.90), channel_id=1, source_target_pairs={{0,8},{4,12},{8,0},{12,4},{16,24},{20,28},{24,16},{28,20},{1,9},{5... | collective-permute-start | bytes 221192 | tf_op jit(solution)/shard_map/ppermute | solution.py:54
  83.5 13.9 %collective-permute-start.16 = (bf16[48,1536]{1,0:T(8,128)(2,1)S(1)}, bf16[48,1536]{1,0:T(8,128)(2,1)S(1)}, u32[]{:S(2)}, u32[]{:S(2)}) collective-permute-start(bf16[48,1536]{1,0:T(8,128)(2,1)S(1)} %fusion.61.refs_0_), channel_id=1, source_target_pairs={{0,2},{1,3},{2,0},{3,1},{4,6},{5,7},{6,4},{7,5},{8,10},{9,11},{10,... | collective-permute-start | bytes 442376 | tf_op jit(solution)/shard_map/ppermute | solution.py:54
  117.8 15.5 %collective-permute-start.30 = (bf16[192,192]{1,0:T(8,128)(2,1)}, bf16[192,192]{1,0:T(8,128)(2,1)S(1)}, u32[]{:S(2)}, u32[]{:S(2)}) collective-permute-start(bf16[192,192]{1,0:T(8,128)(2,1)} %get-tuple-element.89), channel_id=1, source_target_pairs={{0,16},{4,20},{8,24},{12,28},{16,0},{20,4},{24,8},{28,12},{1,17},{... | collective-permute-start | bytes 221192 | tf_op jit(solution)/shard_map/ppermute | solution.py:54
  140.5 23.5 %collective-permute-start.73 = (bf16[192,1536]{1,0:T(8,128)(2,1)}, bf16[192,1536]{1,0:T(8,128)(2,1)S(1)}, u32[]{:S(2)}, u32[]{:S(2)}) collective-permute-start(bf16[192,1536]{1,0:T(8,128)(2,1)} %refs_10_.1), channel_id=1, source_target_pairs={{0,8},{4,12},{8,0},{12,4},{16,24},{20,28},{24,16},{28,20},{1,9},{5... | collective-permute-start | bytes 1769480 | tf_op jit(solution)/shard_map/ppermute | solution.py:54
  142.7 24.2 %collective-permute-start.74 = (bf16[192,1536]{1,0:T(8,128)(2,1)}, bf16[192,1536]{1,0:T(8,128)(2,1)S(1)}, u32[]{:S(2)}, u32[]{:S(2)}) collective-permute-start(bf16[192,1536]{1,0:T(8,128)(2,1)} %refs_10_.1), channel_id=1, source_target_pairs={{0,16},{4,20},{8,24},{12,28},{16,0},{20,4},{24,8},{28,12},{1,17},{... | collective-permute-start | bytes 1769480 | tf_op jit(solution)/shard_map/ppermute | solution.py:54
  143.1 24.6 %collective-permute-start.77 = (bf16[192,1536]{1,0:T(8,128)(2,1)}, bf16[192,1536]{1,0:T(8,128)(2,1)S(1)}, u32[]{:S(2)}, u32[]{:S(2)}) collective-permute-start(bf16[192,1536]{1,0:T(8,128)(2,1)} %refs_10_.1), channel_id=1, source_target_pairs={{0,4},{4,0},{8,12},{12,8},{16,20},{20,16},{24,28},{28,24},{1,5},{5... | collective-permute-start | bytes 1769480 | tf_op jit(solution)/shard_map/ppermute | solution.py:54
  172.7 54.1 %collective-permute-start.64 = (bf16[192,1536]{1,0:T(8,128)(2,1)S(1)}, bf16[192,1536]{1,0:T(8,128)(2,1)S(1)}, u32[]{:S(2)}, u32[]{:S(2)}) collective-permute-start(bf16[192,1536]{1,0:T(8,128)(2,1)S(1)} %copy-done.1), channel_id=1, source_target_pairs={{0,8},{4,12},{8,0},{12,4},{16,24},{20,28},{24,16},{28,20},{1,9},{5... | collective-permute-start | bytes 1769480 | tf_op jit(solution)/shard_map/ppermute | solution.py:54
  174.3 19.0 %collective-permute-start.36 = (bf16[192,640]{1,0:T(8,128)(2,1)S(1)}, bf16[192,640]{1,0:T(8,128)(2,1)S(1)}, u32[]{:S(2)}, u32[]{:S(2)}) collective-permute-start(bf16[192,640]{1,0:T(8,128)(2,1)S(1)} %pad_maximum_fusion.refs_8_), channel_id=1, source_target_pairs={{0,8},{4,12},{8,0},{12,4},{16,24},{20,28},{24,16},{28,20},{1,9},{5... | collective-permute-start | bytes 737288 | tf_op jit(solution)/shard_map/ppermute | solution.py:54
  174.9 18.6 %collective-permute-start.37 = (bf16[192,640]{1,0:T(8,128)(2,1)S(1)}, bf16[192,640]{1,0:T(8,128)(2,1)S(1)}, u32[]{:S(2)}, u32[]{:S(2)}) collective-permute-start(bf16[192,640]{1,0:T(8,128)(2,1)S(1)} %pad_maximum_fusion.refs_8_), channel_id=1, source_target_pairs={{0,16},{4,20},{8,24},{12,28},{16,0},{20,4},{24,8},{28,12},{1,17},{... | collective-permute-start | bytes 737288 | tf_op jit(solution)/shard_map/ppermute | solution.py:54
  175.6 19.8 %collective-permute-start.40 = (bf16[192,640]{1,0:T(8,128)(2,1)S(1)}, bf16[192,640]{1,0:T(8,128)(2,1)S(1)}, u32[]{:S(2)}, u32[]{:S(2)}) collective-permute-start(bf16[192,640]{1,0:T(8,128)(2,1)S(1)} %pad_maximum_fusion.refs_8_), channel_id=1, source_target_pairs={{0,4},{4,0},{8,12},{12,8},{16,20},{20,16},{24,28},{28,24},{1,5},{5... | collective-permute-start | bytes 737288 | tf_op jit(solution)/shard_map/ppermute | solution.py:54
  180.1 22.8 %collective-permute-start.9 = (bf16[48,1536]{1,0:T(8,128)(2,1)S(1)}, bf16[48,1536]{1,0:T(8,128)(2,1)S(1)}, u32[]{:S(2)}, u32[]{:S(2)}) collective-permute-start(bf16[48,1536]{1,0:T(8,128)(2,1)S(1)} %get-tuple-element.107.refs_0_), channel_id=1, source_target_pairs={{0,1},{1,0},{2,3},{3,2},{4,5},{5,4},{6,7},{7,6},{8,9},{9,8},{10,11... | collective-permute-start | bytes 442376 | tf_op jit(solution)/shard_map/ppermute | solution.py:54
  193.5 34.9 %collective-permute-start.65 = (bf16[192,1536]{1,0:T(8,128)(2,1)S(1)}, bf16[192,1536]{1,0:T(8,128)(2,1)}, u32[]{:S(2)}, u32[]{:S(2)}) collective-permute-start(bf16[192,1536]{1,0:T(8,128)(2,1)S(1)} %copy-done.1), channel_id=1, source_target_pairs={{0,16},{4,20},{8,24},{12,28},{16,0},{20,4},{24,8},{28,12},{1,17},{... | collective-permute-start | bytes 1769480 | tf_op jit(solution)/shard_map/ppermute | solution.py:54
  202.9 33.2 %collective-permute-start.68 = (bf16[192,1536]{1,0:T(8,128)(2,1)S(1)}, bf16[192,1536]{1,0:T(8,128)(2,1)S(1)}, u32[]{:S(2)}, u32[]{:S(2)}) collective-permute-start(bf16[192,1536]{1,0:T(8,128)(2,1)S(1)} %copy-done.1), channel_id=1, source_target_pairs={{0,4},{4,0},{8,12},{12,8},{16,20},{20,16},{24,28},{28,24},{1,5},{5... | collective-permute-start | bytes 1769480 | tf_op jit(solution)/shard_map/ppermute | solution.py:54
  236.1 19.1 %collective-permute-start.78 = (bf16[192,1536]{1,0:T(8,128)(2,1)}, bf16[192,1536]{1,0:T(8,128)(2,1)}, u32[]{:S(2)}, u32[]{:S(2)}) collective-permute-start(bf16[192,1536]{1,0:T(8,128)(2,1)} %copy-done.16), channel_id=1, source_target_pairs={{0,4},{4,0},{8,12},{12,8},{16,20},{20,16},{24,28},{28,24},{1,5},{5... | collective-permute-start | bytes 1769480 | tf_op jit(solution)/shard_map/ppermute | solution.py:54
  241.5 19.3 %collective-permute-start.79 = (bf16[192,1536]{1,0:T(8,128)(2,1)S(1)}, bf16[192,1536]{1,0:T(8,128)(2,1)}, u32[]{:S(2)}, u32[]{:S(2)}) collective-permute-start(bf16[192,1536]{1,0:T(8,128)(2,1)S(1)} %copy-done.18), channel_id=1, source_target_pairs={{0,4},{4,0},{8,12},{12,8},{16,20},{20,16},{24,28},{28,24},{1,5},{5... | collective-permute-start | bytes 1769480 | tf_op jit(solution)/shard_map/ppermute | solution.py:54
  244.0 20.0 %collective-permute-start.69 = (bf16[192,1536]{1,0:T(8,128)(2,1)S(1)}, bf16[192,1536]{1,0:T(8,128)(2,1)}, u32[]{:S(2)}, u32[]{:S(2)}) collective-permute-start(bf16[192,1536]{1,0:T(8,128)(2,1)S(1)} %copy-done.20), channel_id=1, source_target_pairs={{0,4},{4,0},{8,12},{12,8},{16,20},{20,16},{24,28},{28,24},{1,5},{5... | collective-permute-start | bytes 1769480 | tf_op jit(solution)/shard_map/ppermute | solution.py:54
  246.2 17.9 %collective-permute-start.70 = (bf16[192,1536]{1,0:T(8,128)(2,1)}, bf16[192,1536]{1,0:T(8,128)(2,1)}, u32[]{:S(2)}, u32[]{:S(2)}) collective-permute-start(bf16[192,1536]{1,0:T(8,128)(2,1)} %collective-permute-done.65.refs_2_), channel_id=1, source_target_pairs={{0,4},{4,0},{8,12},{12,8},{16,20},{20,16},{24,28},{28,24},{1,5},{5... | collective-permute-start | bytes 1769480 | tf_op jit(solution)/shard_map/ppermute | solution.py:54
  247.3 13.6 %collective-permute-start.80 = (bf16[96,1536]{1,0:T(8,128)(2,1)}, bf16[96,1536]{1,0:T(8,128)(2,1)}, u32[]{:S(2)}, u32[]{:S(2)}) collective-permute-start(bf16[96,1536]{1,0:T(8,128)(2,1)} %collective-permute-done.75.refs_13_), channel_id=1, source_target_pairs={{0,4},{4,0},{8,12},{12,8},{16,20},{20,16},{24,28},{28,24},{1,5},{5... | collective-permute-start | bytes 884744 | tf_op jit(solution)/shard_map/ppermute | solution.py:54
  262.0 31.7 %collective-permute-start.47 = (f32[48,256]{1,0:T(8,128)}, f32[48,256]{1,0:T(8,128)S(1)}, u32[]{:S(2)}, u32[]{:S(2)}) collective-permute-start(f32[48,256]{1,0:T(8,128)} %get-tuple-element.115), channel_id=1, source_target_pairs={{0,3},{1,2},{2,1},{3,0},{4,7},{5,6},{6,5},{7,4},{8,11},{9,10},{10,... | collective-permute-start | bytes 147464 | tf_op jit(solution)/shard_map/ppermute | solution.py:54
  264.0 29.6 %collective-permute-start.46 = (f32[48,256]{1,0:T(8,128)S(1)}, f32[48,256]{1,0:T(8,128)S(1)}, u32[]{:S(2)}, u32[]{:S(2)}) collective-permute-start(f32[48,256]{1,0:T(8,128)S(1)} %get-tuple-element.116), channel_id=1, source_target_pairs={{0,2},{1,3},{2,0},{3,1},{4,6},{5,7},{6,4},{7,5},{8,10},{9,11},{10,... | collective-permute-start | bytes 147464 | tf_op jit(solution)/shard_map/ppermute | solution.py:54
  264.1 29.6 %collective-permute-start.45 = (f32[48,256]{1,0:T(8,128)S(1)}, f32[48,256]{1,0:T(8,128)S(1)}, u32[]{:S(2)}, u32[]{:S(2)}) collective-permute-start(f32[48,256]{1,0:T(8,128)S(1)} %get-tuple-element.114), channel_id=1, source_target_pairs={{0,1},{1,0},{2,3},{3,2},{4,5},{5,4},{6,7},{7,6},{8,9},{9,8},{10,11... | collective-permute-start | bytes 147464 | tf_op jit(solution)/shard_map/ppermute | solution.py:54
  293.7 20.3 %collective-permute-start.84 = (bf16[3,280,192]{2,1,0:T(8,128)(2,1)}, bf16[3,280,192]{2,1,0:T(8,128)(2,1)S(1)}, u32[]{:S(2)}, u32[]{:S(2)}) collective-permute-start(bf16[3,280,192]{2,1,0:T(8,128)(2,1)} %get-tuple-element.28), channel_id=1, source_target_pairs={{0,12},{4,8},{8,4},{12,0},{16,28},{20,24},{24,20},{28,16},{1,13},{... | collective-permute-start | bytes 967688 | tf_op jit(solution)/shard_map/ppermute | solution.py:54
  294.8 19.2 %collective-permute-start.85 = (bf16[3,280,192]{2,1,0:T(8,128)(2,1)}, bf16[3,280,192]{2,1,0:T(8,128)(2,1)S(1)}, u32[]{:S(2)}, u32[]{:S(2)}) collective-permute-start(bf16[3,280,192]{2,1,0:T(8,128)(2,1)} %get-tuple-element.29), channel_id=1, source_target_pairs={{0,16},{4,20},{8,24},{12,28},{16,0},{20,4},{24,8},{28,12},{1,17},{... | collective-permute-start | bytes 967688 | tf_op jit(solution)/shard_map/ppermute | solution.py:54
  296.6 37.7 %collective-permute-start.86 = (bf16[3,280,192]{2,1,0:T(8,128)(2,1)}, bf16[3,280,192]{2,1,0:T(8,128)(2,1)}, u32[]{:S(2)}, u32[]{:S(2)}) collective-permute-start(bf16[3,280,192]{2,1,0:T(8,128)(2,1)} %get-tuple-element.30), channel_id=1, source_target_pairs={{0,20},{4,16},{8,28},{12,24},{16,4},{20,0},{24,12},{28,8},{1,21},{... | collective-permute-start | bytes 967688 | tf_op jit(solution)/shard_map/ppermute | solution.py:54
  296.6 37.6 %collective-permute-start.87 = (bf16[3,280,192]{2,1,0:T(8,128)(2,1)}, bf16[3,280,192]{2,1,0:T(8,128)(2,1)}, u32[]{:S(2)}, u32[]{:S(2)}) collective-permute-start(bf16[3,280,192]{2,1,0:T(8,128)(2,1)} %get-tuple-element.31), channel_id=1, source_target_pairs={{0,24},{4,28},{8,16},{12,20},{16,8},{20,12},{24,0},{28,4},{1,25},{... | collective-permute-start | bytes 967688 | tf_op jit(solution)/shard_map/ppermute | solution.py:54
  305.9 28.3 %collective-permute-start.88 = (bf16[3,280,192]{2,1,0:T(8,128)(2,1)}, bf16[3,280,192]{2,1,0:T(8,128)(2,1)}, u32[]{:S(2)}, u32[]{:S(2)}) collective-permute-start(bf16[3,280,192]{2,1,0:T(8,128)(2,1)} %get-tuple-element.32), channel_id=1, source_target_pairs={{0,28},{4,24},{8,20},{12,16},{16,12},{20,8},{24,4},{28,0},{1,29},{... | collective-permute-start | bytes 967688 | tf_op jit(solution)/shard_map/ppermute | solution.py:54
  (168 other events, 1865.2 us)
where the time goes:
time: 345 us; the launch traced here: 343 us
  waiting for transfers between devices  123 us (36%)
  starting transfers between devices  85.2 us (25%)
  local copies, waits for them, and re-layouts  41.4 us (12%)
  Pallas kernels  40.7 us (12%)
  matrix products  32.4 us (9%)
  other arithmetic  18.6 us (5%)
    ppermute x89, waiting for transfers between devices, swap(): lax.ppermute(values, axis, [(rank, rank ^ step) for rank in range(size)])  123 us
    ppermute x89, starting transfers between devices, swap(): lax.ppermute(values, axis, [(rank, rank ^ step) for rank in range(size)])  85.2 us
    dot_general x13, matrix products, dot(): return jnp.dot(a, b, preferred_element_type=f32)  23.5 us
    pallas_call x1, Pallas kernels, slice_grads(): pl.pallas_call(functools.partial(slice_kernel, count, parts), out_shape=[...  19.8 us
    unnamed x228, local copies, waits for them, and re-layouts  16 us
    pallas_call x4, Pallas kernels, arrange(): pl.pallas_call(arrange_kernel, out_shape=jax.ShapeDtypeStruct((parts * si...  8.44 us
  transfers between devices with their start and end apart: 89, of which 31 were waited for; matrix products, arithmetic and copies ran while one was open for 21% of the time, Pallas kernels for 10%

commit v1 on v0

--- a/solution.py
+++ b/solution.py
@@ -54,23 +54,28 @@
     return lax.ppermute(values, axis, [(rank, rank ^ step) for rank in range(size)])
 
 
+def turn(values, first):
+    steps = (2, 4) if first else (4, 2)
+    return lax.ppermute(values, "dp", [(rank, rank ^ steps[rank % 2]) for rank in range(8)])
+
+
 def gather_dp(own):
     parts = lax.axis_size("dp")
-    near, far = [own], []
     if parts == 8:
-        half = own.shape[0] // 2
         along_x = swap(own, "dp", 2)
         along_y = swap(own, "dp", 4)
-        near = [own, along_x, along_y]
-        far = [swap(along_y[:half], "dp", 2), swap(along_x[half:], "dp", 4)]
+        onward = jnp.where(lax.axis_index("dp") % 2 == 0, along_y, along_x)
+        chips = [own, along_x, along_y, turn(onward, True)]
     else:
+        chips = [own]
         step = 2
         while step < parts:
-            near = near + [swap(chip, "dp", step) for chip in near]
+            chips = chips + [swap(chip, "dp", step) for chip in chips]
             step *= 2
-    partner = [swap(chip, "dp", 1) for chip in near]
-    partner += [swap(chip, "dp", 1) for chip in far]
-    return near + far + partner
+    blocks = []
+    for chip in chips:
+        blocks += [chip, swap(chip, "dp", 1)]
+    return blocks
 
 
 VMEM = pl.BlockSpec(memory_space=pltpu.VMEM)
@@ -118,11 +123,10 @@
 def slice_kernel(count, parts, rank, *refs):
     normed_refs, cot_refs = refs[:count], refs[count : 2 * count]
     gate_up, down = refs[2 * count : 2 * count + 2]
-    outs = refs[2 * count + 2 : 2 * count + 2 + parts]
-    normed, cot, wide, narrow, pieces, sems = refs[2 * count + 2 + parts :]
+    keep, give, normed, cot, wide, narrow, pieces, sems = refs[2 * count + 2 :]
     padded = down.shape[0]
     tokens, width = normed.shape
-    _, units, rows = outs[0].shape
+    rows = width // parts
     f32, bf16 = jnp.float32, jnp.bfloat16
     waits = fetch(normed_refs, normed, sems, 0) + fetch(cot_refs, cot, sems, count)
     for copy in waits:
@@ -150,17 +154,18 @@
         last = product(narrow[...], cot[:, at], ((1,), (0,))).astype(bf16)
         for k in range(per):
             cols = slice(k * rows, (k + 1) * rows)
-            pieces[step * per + k, 0] = both[:units, cols]
-            pieces[step * per + k, 1] = both[padded : padded + units, cols]
-            pieces[step * per + k, 2] = last[:units, cols]
+            pieces[step * per + k, : 2 * padded] = both[:, cols]
+            pieces[step * per + k, 2 * padded :] = last[:, cols]
         return carry
 
     lax.fori_loop(0, width // block, backward, 0)
-    for k in range(parts):
-        outs[k][...] = pieces[rank[0] ^ k]
-
-
-def slice_grads(normed_blocks, cot_blocks, gate_up, down, rank, parts, units):
+    for k in range(parts // 2):
+        cols = slice((k % 2) * rows, (k % 2 + 1) * rows)
+        keep[k // 2, :, cols] = pieces[rank[0] ^ (2 * k)]
+        give[k // 2, :, cols] = pieces[rank[0] ^ (2 * k + 1)]
+
+
+def slice_grads(normed_blocks, cot_blocks, gate_up, down, rank, parts):
     count = len(normed_blocks)
     padded, width = down.shape
     tokens = sum(block.shape[0] for block in normed_blocks)
@@ -168,74 +173,132 @@
     bf16 = jnp.bfloat16
     return pl.pallas_call(
         functools.partial(slice_kernel, count, parts),
-        out_shape=[jax.ShapeDtypeStruct((3, units, rows), bf16)] * parts,
+        out_shape=[jax.ShapeDtypeStruct((parts // 4, 3 * padded, 2 * rows), bf16)] * 2,
         in_specs=[SMEM] + [ANY] * (2 * count) + [VMEM, VMEM],
-        out_specs=[VMEM] * parts,
+        out_specs=[VMEM] * 2,
         scratch_shapes=[
             pltpu.VMEM((tokens, width), bf16),
             pltpu.VMEM((tokens, width), bf16),
             pltpu.VMEM((2 * padded, tokens), bf16),
             pltpu.VMEM((padded, tokens), bf16),
-            pltpu.VMEM((parts, 3, units, rows), bf16),
+            pltpu.VMEM((parts, 3 * padded, rows), bf16),
             pltpu.SemaphoreType.DMA((2 * count,)),
         ],
         name="slice_grads",
     )(rank.reshape(1), *normed_blocks, *cot_blocks, gate_up, down)
 
 
-def place_kernel(rank, *refs):
-    parts = len(refs) - 4
-    pieces, (gate_out, up_out, down_out, buffer) = refs[:parts], refs[parts:]
-    units = pieces[0].shape[1]
-    for k in range(parts):
-        buffer[rank[0] ^ k] = pieces[k][...]
+def pack_kernel(rank, keep, given, own, partner, *refs):
+    messages, own_cols, partner_cols = refs[:-2], refs[-2], refs[-1]
+    parts, _, rows = own_cols.shape
+    size = keep.shape[1]
     for j in range(parts):
-        gate_out[:, j * units : (j + 1) * units] = buffer[j, 0].astype(jnp.float32).T
-        up_out[:, j * units : (j + 1) * units] = buffer[j, 1].astype(jnp.float32).T
-        down_out[j * units : (j + 1) * units, :] = buffer[j, 2].astype(jnp.float32)
-
-
-def place(pieces, rank):
-    parts = len(pieces)
-    _, units, rows = pieces[0].shape
+        own_cols[j] = own[:, j * rows : (j + 1) * rows]
+        partner_cols[j] = partner[:, j * rows : (j + 1) * rows]
+    for k, message in enumerate(messages):
+        cols = slice((k % 2) * rows, (k % 2 + 1) * rows)
+        message[:size, :rows] = keep[k // 2, :, cols]
+        message[:size, rows:] = given[k // 2, :, cols]
+        message[size:, :rows] = own_cols[rank[0] ^ (2 * k)]
+        message[size:, rows:] = partner_cols[rank[0] ^ (2 * k)]
+
+
+def pack(keep, given, own, partner, rank):
+    pairs, size, wide = keep.shape
+    tokens = own.shape[0]
+    bf16 = jnp.bfloat16
+    return pl.pallas_call(
+        pack_kernel,
+        out_shape=[jax.ShapeDtypeStruct((size + tokens, wide), bf16)] * (2 * pairs),
+        in_specs=[SMEM] + [VMEM] * 4,
+        out_specs=[VMEM] * (2 * pairs),
+        scratch_shapes=[pltpu.VMEM((4 * pairs, tokens, wide // 2), bf16)] * 2,
+        name="pack",
+    )(rank.reshape(1), keep, given, own, partner)
+
+
+def place_kernel(padded, rank, *refs):
+    messages, (gate_out, up_out, down_out, buffer) = refs[:-4], refs[-4:]
+    parts = 2 * len(messages)
+    units = gate_out.shape[1] // parts
+    rows = gate_out.shape[0]
+    size = 3 * padded
+    for k, message in enumerate(messages):
+        buffer[rank[0] ^ (2 * k)] = message[:size, :rows]
+        buffer[rank[0] ^ (2 * k + 1)] = message[:size, rows:]
+    for j in range(parts):
+        for part, out in enumerate((gate_out, up_out, down_out)):
+            piece = buffer[j, part * padded : (part + 1) * padded].astype(jnp.float32).T
+            out[:, j * units : (j + 1) * units] = piece[:, :units]
+
+
+def place(messages, rank, units, padded):
+    parts = 2 * len(messages)
+    rows = messages[0].shape[1] // 2
     wide = jax.ShapeDtypeStruct((rows, parts * units), jnp.float32)
-    tall = jax.ShapeDtypeStruct((parts * units, rows), jnp.float32)
     return pl.pallas_call(
-        place_kernel,
-        out_shape=(wide, wide, tall),
-        in_specs=[SMEM] + [VMEM] * parts,
+        functools.partial(place_kernel, padded),
+        out_shape=(wide, wide, wide),
+        in_specs=[SMEM] + [VMEM] * len(messages),
         out_specs=(VMEM, VMEM, VMEM),
-        scratch_shapes=[pltpu.VMEM((parts,) + pieces[0].shape, jnp.bfloat16)],
+        scratch_shapes=[pltpu.VMEM((parts, 3 * padded, rows), jnp.bfloat16)],
         name="place",
-    )(rank.reshape(1), *pieces)
-
-
-def outer_kernel(left_count, right_count, *refs):
-    left_refs = refs[:left_count]
-    right_refs = refs[left_count : left_count + right_count]
-    out, left, right, sems = refs[left_count + right_count :]
-    waits = fetch(left_refs, left, sems, 0) + fetch(right_refs, right, sems, left_count)
-    for copy in waits:
+    )(rank.reshape(1), *messages)
+
+
+def outer_kernel(left_count, *refs):
+    left_refs, right_refs, (out, left, right, sems) = refs[:left_count], refs[left_count:-4], refs[-4:]
+    for copy in fetch(left_refs, left, sems, 0) + fetch(right_refs, right, sems, left_count):
         copy.wait()
     out[...] = product(left[...], right[...], ((0,), (0,)))
 
 
 def outer(left_blocks, right_blocks):
-    tokens = sum(block.shape[0] for block in left_blocks)
+    tokens = sum(block.shape[0] for block in right_blocks)
     left_width, right_width = left_blocks[0].shape[1], right_blocks[0].shape[1]
-    counts = (len(left_blocks), len(right_blocks))
+    count = len(left_blocks) + len(right_blocks)
     return pl.pallas_call(
-        functools.partial(outer_kernel, *counts),
+        functools.partial(outer_kernel, len(left_blocks)),
         out_shape=jax.ShapeDtypeStruct((left_width, right_width), jnp.float32),
-        in_specs=[ANY] * sum(counts),
+        in_specs=[ANY] * count,
         out_specs=VMEM,
         scratch_shapes=[
             pltpu.VMEM((tokens, left_width), jnp.bfloat16),
             pltpu.VMEM((tokens, right_width), jnp.bfloat16),
-            pltpu.SemaphoreType.DMA((sum(counts),)),
+            pltpu.SemaphoreType.DMA((count,)),
         ],
         name="outer",
     )(*left_blocks, *right_blocks)
+
+
+def outer_message_kernel(first_row, count, *refs):
+    messages, right_refs, (out, left, right, sems) = refs[:count], refs[count:-4], refs[-4:]
+    waits = fetch(right_refs, right, sems, 0)
+    tokens = messages[0].shape[0] - first_row
+    width = left.shape[1]
+    for k, message in enumerate(messages):
+        left[2 * k * tokens : (2 * k + 1) * tokens] = message[first_row:, :width]
+        left[(2 * k + 1) * tokens : (2 * k + 2) * tokens] = message[first_row:, width:]
+    for copy in waits:
+        copy.wait()
+    out[...] = product(left[...], right[...], ((0,), (0,)))
+
+
+def outer_message(messages, first_row, right_blocks):
+    tokens = sum(block.shape[0] for block in right_blocks)
+    left_width, right_width = messages[0].shape[1] // 2, right_blocks[0].shape[1]
+    return pl.pallas_call(
+        functools.partial(outer_message_kernel, first_row, len(messages)),
+        out_shape=jax.ShapeDtypeStruct((left_width, right_width), jnp.float32),
+        in_specs=[VMEM] * len(messages) + [ANY] * len(right_blocks),
+        out_specs=VMEM,
+        scratch_shapes=[
+            pltpu.VMEM((tokens, left_width), jnp.bfloat16),
+            pltpu.VMEM((tokens, right_width), jnp.bfloat16),
+            pltpu.SemaphoreType.DMA((len(right_blocks),)),
+        ],
+        name="outer",
+    )(*messages, *right_blocks)
 
 
 def local(
@@ -272,7 +335,7 @@
 
     def exchange_columns(values):
         blocks = []
-        for k in [*range(0, dp, 2), *range(1, dp, 2)]:
+        for k in range(dp):
             block = lax.dynamic_slice_in_dim(values, (dp_rank ^ k) * slice_rows, slice_rows, 1)
             blocks.append(swap(block, "dp", k) if k else block)
         return blocks
@@ -360,14 +423,20 @@
     d_hidden = own_block(cot).astype(f32) + norm_back(hidden, rscale_mlp, gain_mlp, d_normed_mlp)
     d_hidden_own = d_hidden.astype(bf16)
     d_hidden_b = arrange(d_hidden_own, "tensor", tp_rank, bf16)
-    output_own = hidden + reduce_tensor(out_partial)
-    output = arrange(output_own.astype(bf16), "tensor", tp_rank, f32)
-
-    pieces = slice_grads(normed_blocks, cot_blocks, gate_up, down_slice, dp_rank, dp, units)
-    pieces = [swap(piece, "dp", k) if k else piece for k, piece in enumerate(pieces)]
-    summed_gate, summed_up, summed_down = place(pieces, dp_rank)
-    d_hidden_slices = exchange_columns(d_hidden_b)
-    summed_out = outer(heads_blocks, d_hidden_slices)
+    out_total = reduce_tensor(out_partial)
+
+    keep, give = slice_grads(normed_blocks, cot_blocks, gate_up, down_slice, dp_rank, dp)
+    given = swap(give, "dp", 1)
+    partner_hidden = swap(d_hidden_b, "dp", 1)
+    packed = pack(keep, given, d_hidden_b, partner_hidden, dp_rank)
+    messages = [packed[0]]
+    for k in range(1, dp // 2):
+        if dp == 8 and k == 3:
+            messages.append(turn(turn(packed[k], True), False))
+        else:
+            messages.append(swap(packed[k], "dp", 2 * k))
+    summed_gate, summed_up, down_columns = place(messages, dp_rank, units, down_slice.shape[0])
+    summed_out = outer_message(messages, keep.shape[1], heads_blocks).T
 
     d_heads = dot(d_hidden_b, w_out.T).astype(bf16).reshape(row_count, local_heads, HD)
     d_probs = jnp.einsum("thd,ud->htu", d_heads, value_heads, preferred_element_type=f32)
@@ -386,7 +455,10 @@
     factor_blocks = gather_dp(jnp.concatenate([query_grad, key_grad, value_grad], axis=1))
     grad_gain_attn = jnp.sum(d_normed_attn * input_own * rscale_own, axis=0)
     d_input_own = d_hidden + norm_back(input_own, rscale_own, gain_attn, d_normed_attn)
-    d_input = arrange(d_input_own.astype(bf16), "tensor", tp_rank, f32)
+    d_input_b = lax.optimization_barrier(d_input_own.astype(bf16))
+    d_input = arrange(d_input_b, "tensor", tp_rank, f32)
+    out_total, _ = lax.optimization_barrier((out_total, d_input_b))
+    output = arrange((hidden + out_total).astype(bf16), "tensor", tp_rank, f32)
 
     products = outer(normed_slice, factor_blocks)
     summed_query = products[:, : local_heads * HD]
@@ -438,7 +510,7 @@
         gain_mlp_sum,
         summed_gate,
         summed_up,
-        summed_down,
+        down_columns.T,
     )
 
 

time: 345 us -> 299 us (0.87)
  waiting for transfers between devices: 123 us -> 57.7 us
  other arithmetic: 18.6 us -> 34.1 us
  Pallas kernels: 40.7 us -> 47.1 us
  starting transfers between devices: 85.2 us -> 79.5 us
  matrix products: 32.4 us -> 36.4 us
    ppermute x89 -> x67, waiting for transfers between devices: 123 us -> 42 us  [swap(): lax.ppermute(values, axis, [(rank, rank ^ step) for rank in range(size)])]
    ppermute x0 -> x6, waiting for transfers between devices: none -> 15.8 us  [turn(): lax.ppermute(values, 'dp', [(rank, rank ^ steps[rank % 2]) for rank in ra...]
    ppermute x89 -> x67, starting transfers between devices: 85.2 us -> 73.8 us  [swap(): lax.ppermute(values, axis, [(rank, rank ^ step) for rank in range(size)])]
    pallas_call x3 -> x4, Pallas kernels: 12.5 us -> 19.1 us  [the longest x1 6.84 us: place(): pl.pallas_call(functools.partial(place_kernel, padded), out_shape=(wide,...]
    select_n x0 -> x4, other arithmetic: none -> 6.27 us  [gather_dp(): onward = jnp.where(lax.axis_index('dp') % 2 == 0, along_y, along_x)]
    slice x8 -> x0, local copies, waits for them, and re-layouts: 6.18 us -> none  [gather_dp(): far = [swap(along_y[:half], 'dp', 2), swap(along_x[half:], 'dp', 4)]]
    ppermute x0 -> x6, starting transfers between devices: none -> 5.66 us  [turn(): lax.ppermute(values, 'dp', [(rank, rank ^ steps[rank % 2]) for rank in ra...]
    dot_general x13, matrix products: 23.5 us -> 28.1 us  [dot(): return jnp.dot(a, b, preferred_element_type=f32)]
  transfers between devices with their start and end apart: 89 -> 73, of which waited for: 31 -> 17; matrix products, arithmetic and copies ran while one was open for 21% -> 34% of each run, Pallas kernels for 10% -> 14%
where the time goes in v1:
time: 299 us; the launch traced here: 297 us
  starting transfers between devices  79.5 us (27%)
  waiting for transfers between devices  57.7 us (19%)
  Pallas kernels  47.1 us (16%)
  local copies, waits for them, and re-layouts  40.2 us (13%)
  matrix products  36.4 us (12%)
  other arithmetic  34.1 us (11%)
    ppermute x67, starting transfers between devices, swap(): lax.ppermute(values, axis, [(rank, rank ^ step) for rank in range(size)])  73.8 us
    ppermute x67, waiting for transfers between devices, swap(): lax.ppermute(values, axis, [(rank, rank ^ step) for rank in range(size)])  42 us
    dot_general x13, matrix products, dot(): return jnp.dot(a, b, preferred_element_type=f32)  28.1 us
    pallas_call x1, Pallas kernels, slice_grads(): pl.pallas_call(functools.partial(slice_kernel, count, parts), out_shape=[...  19.7 us
    unnamed x196, local copies, waits for them, and re-layouts  16.1 us
    ppermute x6, waiting for transfers between devices, turn(): lax.ppermute(values, 'dp', [(rank, rank ^ steps[rank % 2]) for rank in ra...  15.8 us
    pallas_call x4, Pallas kernels, arrange(): pl.pallas_call(arrange_kernel, out_shape=jax.ShapeDtypeStruct((parts * si...  8.4 us
    pallas_call x1, Pallas kernels, place(): pl.pallas_call(functools.partial(place_kernel, padded), out_shape=(wide,...  6.84 us
  transfers between devices with their start and end apart: 73, of which 17 were waited for; matrix products, arithmetic and copies ran while one was open for 34% of the time, Pallas kernels for 14%

profile of v1, /device:TPU:0, one launch (start us, length us, event | category | flops | bytes accessed | tf_op | source)
XLA Modules:
  0.0 297.0 jit_solution(2079324923485430284)
XLA Ops:
  1.2 2.6 collective-permute-start.54
  17.3 3.6 %collective-permute-start.2 = (bf16[48,1536]{1,0:T(8,128)(2,1)}, bf16[48,1536]{1,0:T(8,128)(2,1)S(1)}, u32[]{:S(2)}, u32[]{:S(2)}) collective-permute-start(bf16[48,1536]{1,0:T(8,128)(2,1)} %get-tuple-element.64), channel_id=1, source_target_pairs={{0,3},{1,2},{2,1},{3,0},{4,7},{5,6},{6,5},{7,4},{8,11},{9,10},{10,... | collective-permute-start | bytes 442376 | tf_op jit(solution)/shard_map/ppermute | solution.py:54
  22.9 6.4 %convolution_convert_fusion = bf16[192,2240]{1,0:T(8,128)(2,1)} fusion(bf16[192,1536]{1,0:T(8,128)(2,1)} %refs_8_.1, bf16[2240,1536]{1,0:T(8,128)(2,1)} %param.31), kind=kOutput, calls=%fused_computation | convolution fusion | flops 1321635840 | bytes 8331264 | tf_op jit(solution)/shard_map/dot_general | solution.py:393
  36.3 3.0 %collective-permute-start.4 = (bf16[48,1536]{1,0:T(8,128)(2,1)S(1)}, bf16[48,1536]{1,0:T(8,128)(2,1)S(1)}, u32[]{:S(2)}, u32[]{:S(2)}) collective-permute-start(bf16[48,1536]{1,0:T(8,128)(2,1)S(1)} %multiply_convert_fusion.3.refs_0_), channel_id=1, source_target_pairs={{0,2},{1,3},{2,0},{3,1},{4,6},{5,7},{6,4},{7,5},{8,10},{9,11},{10,... | collective-permute-start | bytes 442376 | tf_op jit(solution)/shard_map/ppermute | solution.py:54
  43.6 6.6 %collective-permute-done.4.refs_2_ = bf16[48,1536]{1,0:T(8,128)(2,1)S(1)} collective-permute-done((bf16[48,1536]{1,0:T(8,128)(2,1)S(1)}, bf16[48,1536]{1,0:T(8,128)(2,1)S(1)}, u32[]{:S(2)}, u32[]{:S(2)}) %collective-permute-start.4) | collective-permute-done | bytes 147488 | tf_op jit(solution)/shard_map/ppermute | solution.py:54
  52.9 5.6 %fusion.71 = f32[192,2240]{1,0:T(8,128)S(1)} fusion(bf16[192,1536]{1,0:T(8,128)(2,1)} %arrange.4.refs_0_, bf16[1536,2240]{0,1:T(8,128)(2,1)} %param.30), kind=kOutput, calls=%fused_computation.184 | convolution fusion | flops 1321205760 | bytes 9191424 | tf_op jit(solution)/shard_map/dot_general | solution.py:344
  58.5 5.9 %fusion.70 = f32[192,2240]{1,0:T(8,128)S(1)} fusion(bf16[192,1536]{1,0:T(8,128)(2,1)S(1)} %copy-done.1, bf16[1536,2240]{0,1:T(8,128)(2,1)} %param.29), kind=kOutput, calls=%fused_computation.183 | convolution fusion | flops 1321205760 | bytes 9191424 | tf_op jit(solution)/shard_map/dot_general | solution.py:344
  66.9 2.6 fusion.68
  79.6 5.0 %collective-permute-done.10 = bf16[48,1536]{1,0:T(8,128)(2,1)} collective-permute-done((bf16[48,1536]{1,0:T(8,128)(2,1)}, bf16[48,1536]{1,0:T(8,128)(2,1)}, u32[]{:S(2)}, u32[]{:S(2)}) %collective-permute-start.10) | collective-permute-done | bytes 147488 | tf_op jit(solution)/shard_map/ppermute | solution.py:54
  88.2 3.1 %collective-permute-start.13 = (bf16[48,1536]{1,0:T(8,128)(2,1)S(1)}, bf16[48,1536]{1,0:T(8,128)(2,1)S(1)}, u32[]{:S(2)}, u32[]{:S(2)}) collective-permute-start(bf16[48,1536]{1,0:T(8,128)(2,1)S(1)} %fusion.61.refs_0_), channel_id=1, source_target_pairs={{0,2},{1,3},{2,0},{3,1},{4,6},{5,7},{6,4},{7,5},{8,10},{9,11},{10,... | collective-permute-start | bytes 442376 | tf_op jit(solution)/shard_map/ppermute | solution.py:54
  92.6 4.6 %fusion.17 = f32[192,1536]{1,0:T(8,128)S(1)} fusion(bf16[2240,1536]{1,0:T(8,128)(2,1)} %param.31, f32[192,2240]{1,0:T(8,128)S(1)} %copy-done.20, f32[192,2240]{1,0:T(8,128)S(1)} %copy-done.22), kind=kOutput, calls=%fused_computation.38 | convolution fusion | flops 1323786240 | bytes 11501568 | tf_op jit(solution)/shard_map/dot_general | solution.py:344
  115.5 2.4 collective-permute-start.17
  120.5 3.8 %collective-permute-done.49.refs_4_ = bf16[192,1536]{1,0:T(8,128)(2,1)} collective-permute-done((bf16[192,1536]{1,0:T(8,128)(2,1)S(1)}, bf16[192,1536]{1,0:T(8,128)(2,1)}, u32[]{:S(2)}, u32[]{:S(2)}) %collective-permute-start.49) | collective-permute-done | bytes 589856 | tf_op jit(solution)/shard_map/ppermute | solution.py:54
  132.5 2.3 collective-permute-start.15
  135.5 3.1 %collective-permute-done.15 = bf16[48,1536]{1,0:T(8,128)(2,1)S(1)} collective-permute-done((bf16[48,1536]{1,0:T(8,128)(2,1)S(1)}, bf16[48,1536]{1,0:T(8,128)(2,1)S(1)}, u32[]{:S(2)}, u32[]{:S(2)}) %collective-permute-start.15) | collective-permute-done | bytes 147488 | tf_op jit(solution)/shard_map/ppermute | solution.py:54
  138.6 2.5 multiply_reduce_fusion.2
  153.2 19.7 %slice_grads.1 = (bf16[2,864,384]{2,1,0:T(8,128)(2,1)}, bf16[2,864,384]{2,1,0:T(8,128)(2,1)}) custom-call(s32[1]{0:T(128)} %bitcast.19.rank, bf16[192,1536]{1,0:T(8,128)(2,1)} %arrange.4.refs_0_, bf16[192,1536]{1,0:T(8,128)(2,1)} %copy-done.36, bf16[192,1536]{1,0:T(8,128)(2,1)} %collective-permute-done.47.refs_2_, bf16[192,1536]{1,0:T(8,128)(2,1)} %copy-done.38, ...), custom_call_target="tpu_custom_call" | custom-call | tf_op jit(solution)/shard_map/slice_grads/pallas_call | solution.py:174
  176.8 2.9 collective-permute-start.8
  182.9 2.7 collective-permute-done.8
  185.9 6.9 %collective-permute-done.7 = bf16[48,1536]{1,0:T(8,128)(2,1)S(1)} collective-permute-done((bf16[48,1536]{1,0:T(8,128)(2,1)}, bf16[48,1536]{1,0:T(8,128)(2,1)S(1)}, u32[]{:S(2)}, u32[]{:S(2)}) %collective-permute-start.7) | collective-permute-done | bytes 147488 | tf_op jit(solution)/shard_map/ppermute | solution.py:54
  197.9 3.6 %collective-permute-done.32.refs_4_ = bf16[192,192]{1,0:T(8,128)(2,1)S(1)} collective-permute-done((bf16[192,192]{1,0:T(8,128)(2,1)}, bf16[192,192]{1,0:T(8,128)(2,1)S(1)}, u32[]{:S(2)}, u32[]{:S(2)}) %collective-permute-start.32) | collective-permute-done | bytes 73760 | tf_op jit(solution)/shard_map/ppermute | solution.py:54
  204.8 2.4 collective-permute-done.33.refs_5_
  208.2 2.3 collective-permute-start.69
  214.8 4.3 %pack.1 = (bf16[1056,384]{1,0:T(8,128)(2,1)}, bf16[1056,384]{1,0:T(8,128)(2,1)}, bf16[1056,384]{1,0:T(8,128)(2,1)}, bf16[1056,384]{1,0:T(8,128)(2,1)}) custom-call(s32[1]{0:T(128)} %bitcast.19.rank, bf16[2,864,384]{2,1,0:T(8,128)(2,1)} %get-tuple-element.25.keep, bf16[2,864,384]{2,1,0:T(8,128)(2,1)} %copy-done.25, bf16[192,1536]{1,0:T(8,128)(2,1)} %arrange.5.own, ...), custom_call_target="tpu_custom_call" | custom-call | tf_op jit(solution)/shard_map/pack/pallas_call | solution.py:210
  219.1 2.4 collective-permute-start.28
  231.4 3.4 %outer.2 = f32[192,640]{1,0:T(8,128)} custom-call(bf16[192,192]{1,0:T(8,128)(2,1)} %get-tuple-element.53.refs_0_, bf16[192,192]{1,0:T(8,128)(2,1)} %collective-permute-done.29.refs_1_, bf16[192,192]{1,0:T(8,128)(2,1)} %collective-permute-done.30.refs_2_, bf16[192,192]{1,0:T(8,128)(2,1)} %collective-permute-done.31.refs_3_, bf16[192,192]{1,0:T(8,128)(2,1)} %copy-done.76, ...), custom_call_target="tpu_custom_call" | custom-call | tf_op jit(solution)/shard_map/outer/pallas_call | solution.py:260
  236.4 2.5 collective-permute-start.22
  243.7 8.5 %collective-permute-start.44 = (f32[48,256]{1,0:T(8,128)}, f32[48,256]{1,0:T(8,128)S(1)}, u32[]{:S(2)}, u32[]{:S(2)}) collective-permute-start(f32[48,256]{1,0:T(8,128)} %get-tuple-element.76), channel_id=1, source_target_pairs={{0,2},{1,3},{2,0},{3,1},{4,6},{5,7},{6,4},{7,5},{8,10},{9,11},{10,... | collective-permute-start | bytes 147464 | tf_op jit(solution)/shard_map/ppermute | solution.py:54
  267.0 11.4 %collective-permute-done.71.refs_10_ = bf16[192,384]{1,0:T(8,128)(2,1)S(1)} collective-permute-done((bf16[192,384]{1,0:T(8,128)(2,1)}, bf16[192,384]{1,0:T(8,128)(2,1)S(1)}, u32[]{:S(2)}, u32[]{:S(2)}) %collective-permute-start.71) | collective-permute-done | bytes 147488 | tf_op jit(solution)/shard_map/ppermute | solution.py:59
  280.3 4.4 %collective-permute-done.65.refs_3_ = bf16[1056,384]{1,0:T(8,128)(2,1)} collective-permute-done((bf16[1056,384]{1,0:T(8,128)(2,1)}, bf16[1056,384]{1,0:T(8,128)(2,1)}, u32[]{:S(2)}, u32[]{:S(2)}) %collective-permute-start.65) | collective-permute-done | bytes 811040 | tf_op jit(solution)/shard_map/ppermute | solution.py:59
  284.7 6.8 %place.1 = (f32[192,2240]{1,0:T(8,128)}, f32[192,2240]{1,0:T(8,128)}, f32[192,2240]{1,0:T(8,128)}) custom-call(s32[1]{0:T(128)} %bitcast.19.rank, bf16[1056,384]{1,0:T(8,128)(2,1)} %get-tuple-element.27.refs_0_, bf16[1056,384]{1,0:T(8,128)(2,1)} %copy-done.6, bf16[1056,384]{1,0:T(8,128)(2,1)} %copy-done.7, bf16[1056,384]{1,0:T(8,128)(2,1)} %collective-permute-done.65.refs_3_), custom_call_target="tpu_custom_call" | custom-call | tf_op jit(solution)/shard_map/place/pallas_call | solution.py:239
  292.3 4.5 %outer.3 = f32[192,384]{1,0:T(8,128)} custom-call(bf16[1056,384]{1,0:T(8,128)(2,1)} %get-tuple-element.27.refs_0_, bf16[1056,384]{1,0:T(8,128)(2,1)} %copy-done.6, bf16[1056,384]{1,0:T(8,128)(2,1)} %copy-done.7, bf16[1056,384]{1,0:T(8,128)(2,1)} %collective-permute-done.65.refs_3_, bf16[192,384]{1,0:T(8,128)(2,1)} %copy_bitcast_fusion.2.refs_4_, ...), custom_call_target="tpu_custom_call" | custom-call | tf_op jit(solution)/shard_map/outer/pallas_call | solution.py:290
  (416 shorter events, 143.2 us)
Async XLA Ops:
  0.7 125.6 %collective-permute-start.53 = (bf16[192,1536]{1,0:T(8,128)(2,1)}, bf16[192,1536]{1,0:T(8,128)(2,1)}, u32[]{:S(2)}, u32[]{:S(2)}) collective-permute-start(bf16[192,1536]{1,0:T(8,128)(2,1)} %refs_8_.1), channel_id=1, source_target_pairs={{0,4},{4,0},{8,12},{12,8},{16,20},{20,16},{24,28},{28,24},{1,5},{5... | collective-permute-start | bytes 1769480 | tf_op jit(solution)/shard_map/ppermute | solution.py:54
  1.2 114.2 %collective-permute-start.54 = (bf16[192,1536]{1,0:T(8,128)(2,1)}, bf16[192,1536]{1,0:T(8,128)(2,1)}, u32[]{:S(2)}, u32[]{:S(2)}) collective-permute-start(bf16[192,1536]{1,0:T(8,128)(2,1)} %refs_8_.1), channel_id=1, source_target_pairs={{0,8},{4,12},{8,0},{12,4},{16,24},{20,28},{24,16},{28,20},{1,9},{5... | collective-permute-start | bytes 1769480 | tf_op jit(solution)/shard_map/ppermute | solution.py:54
  17.3 14.8 %collective-permute-start.2 = (bf16[48,1536]{1,0:T(8,128)(2,1)}, bf16[48,1536]{1,0:T(8,128)(2,1)S(1)}, u32[]{:S(2)}, u32[]{:S(2)}) collective-permute-start(bf16[48,1536]{1,0:T(8,128)(2,1)} %get-tuple-element.64), channel_id=1, source_target_pairs={{0,3},{1,2},{2,1},{3,0},{4,7},{5,6},{6,5},{7,4},{8,11},{9,10},{10,... | collective-permute-start | bytes 442376 | tf_op jit(solution)/shard_map/ppermute | solution.py:54
  36.3 13.9 %collective-permute-start.4 = (bf16[48,1536]{1,0:T(8,128)(2,1)S(1)}, bf16[48,1536]{1,0:T(8,128)(2,1)S(1)}, u32[]{:S(2)}, u32[]{:S(2)}) collective-permute-start(bf16[48,1536]{1,0:T(8,128)(2,1)S(1)} %multiply_convert_fusion.3.refs_0_), channel_id=1, source_target_pairs={{0,2},{1,3},{2,0},{3,1},{4,6},{5,7},{6,4},{7,5},{8,10},{9,11},{10,... | collective-permute-start | bytes 442376 | tf_op jit(solution)/shard_map/ppermute | solution.py:54
  88.2 13.8 %collective-permute-start.13 = (bf16[48,1536]{1,0:T(8,128)(2,1)S(1)}, bf16[48,1536]{1,0:T(8,128)(2,1)S(1)}, u32[]{:S(2)}, u32[]{:S(2)}) collective-permute-start(bf16[48,1536]{1,0:T(8,128)(2,1)S(1)} %fusion.61.refs_0_), channel_id=1, source_target_pairs={{0,2},{1,3},{2,0},{3,1},{4,6},{5,7},{6,4},{7,5},{8,10},{9,11},{10,... | collective-permute-start | bytes 442376 | tf_op jit(solution)/shard_map/ppermute | solution.py:54
  98.2 17.2 %collective-permute-start.56 = (bf16[192,1536]{1,0:T(8,128)(2,1)}, bf16[192,1536]{1,0:T(8,128)(2,1)}, u32[]{:S(2)}, u32[]{:S(2)}) collective-permute-start(bf16[192,1536]{1,0:T(8,128)(2,1)} %refs_8_.1), channel_id=1, source_target_pairs={{0,16},{4,20},{8,24},{12,28},{16,0},{20,4},{24,8},{28,12},{1,17},{... | collective-permute-start | bytes 1769480 | tf_op jit(solution)/shard_map/ppermute | solution.py:54
  102.1 17.8 %collective-permute-start.47 = (bf16[192,1536]{1,0:T(8,128)(2,1)S(1)}, bf16[192,1536]{1,0:T(8,128)(2,1)}, u32[]{:S(2)}, u32[]{:S(2)}) collective-permute-start(bf16[192,1536]{1,0:T(8,128)(2,1)S(1)} %copy-done.1), channel_id=1, source_target_pairs={{0,8},{4,12},{8,0},{12,4},{16,24},{20,28},{24,16},{28,20},{1,9},{5... | collective-permute-start | bytes 1769480 | tf_op jit(solution)/shard_map/ppermute | solution.py:54
  103.4 20.9 %collective-permute-start.49 = (bf16[192,1536]{1,0:T(8,128)(2,1)S(1)}, bf16[192,1536]{1,0:T(8,128)(2,1)}, u32[]{:S(2)}, u32[]{:S(2)}) collective-permute-start(bf16[192,1536]{1,0:T(8,128)(2,1)S(1)} %copy-done.1), channel_id=1, source_target_pairs={{0,16},{4,20},{8,24},{12,28},{16,0},{20,4},{24,8},{28,12},{1,17},{... | collective-permute-start | bytes 1769480 | tf_op jit(solution)/shard_map/ppermute | solution.py:54
  115.5 27.0 %collective-permute-start.46 = (bf16[192,1536]{1,0:T(8,128)(2,1)S(1)}, bf16[192,1536]{1,0:T(8,128)(2,1)S(1)}, u32[]{:S(2)}, u32[]{:S(2)}) collective-permute-start(bf16[192,1536]{1,0:T(8,128)(2,1)S(1)} %copy-done.1), channel_id=1, source_target_pairs={{0,4},{4,0},{8,12},{12,8},{16,20},{20,16},{24,28},{28,24},{1,5},{5... | collective-permute-start | bytes 1769480 | tf_op jit(solution)/shard_map/ppermute | solution.py:54
  124.3 18.8 %collective-permute-start.58 = (bf16[192,1536]{1,0:T(8,128)(2,1)}, bf16[192,1536]{1,0:T(8,128)(2,1)}, u32[]{:S(2)}, u32[]{:S(2)}) collective-permute-start(bf16[192,1536]{1,0:T(8,128)(2,1)} %broadcast_select_fusion), channel_id=1, source_target_pairs={{0,8},{4,20},{8,0},{12,28},{16,24},{20,4},{24,16},{28,12},{1,9},{5... | collective-permute-start | bytes 1769480 | tf_op jit(solution)/shard_map/ppermute | solution.py:59
  126.3 16.6 %collective-permute-start.55 = (bf16[192,1536]{1,0:T(8,128)(2,1)}, bf16[192,1536]{1,0:T(8,128)(2,1)}, u32[]{:S(2)}, u32[]{:S(2)}) collective-permute-start(bf16[192,1536]{1,0:T(8,128)(2,1)} %collective-permute-done.54.refs_10_), channel_id=1, source_target_pairs={{0,4},{4,0},{8,12},{12,8},{16,20},{20,16},{24,28},{28,24},{1,5},{5... | collective-permute-start | bytes 1769480 | tf_op jit(solution)/shard_map/ppermute | solution.py:54
  126.3 17.2 %collective-permute-start.51 = (bf16[192,1536]{1,0:T(8,128)(2,1)}, bf16[192,1536]{1,0:T(8,128)(2,1)}, u32[]{:S(2)}, u32[]{:S(2)}) collective-permute-start(bf16[192,1536]{1,0:T(8,128)(2,1)} %broadcast_select_fusion.1), channel_id=1, source_target_pairs={{0,8},{4,20},{8,0},{12,28},{16,24},{20,4},{24,16},{28,12},{1,9},{5... | collective-permute-start | bytes 1769480 | tf_op jit(solution)/shard_map/ppermute | solution.py:59
  148.7 24.3 %collective-permute-start.24 = (f32[40,128]{1,0:T(8,128)}, f32[40,128]{1,0:T(8,128)}, u32[]{:S(2)}, u32[]{:S(2)}) collective-permute-start(f32[40,128]{1,0:T(8,128)} %bitcast.164), channel_id=1, source_target_pairs={{0,4},{4,0},{8,12},{12,8},{16,20},{20,16},{24,28},{28,24},{1,5},{5... | collective-permute-start | bytes 61448 | tf_op jit(solution)/shard_map/ppermute | solution.py:54
  149.8 27.0 %collective-permute-start.29 = (bf16[192,192]{1,0:T(8,128)(2,1)}, bf16[192,192]{1,0:T(8,128)(2,1)}, u32[]{:S(2)}, u32[]{:S(2)}) collective-permute-start(bf16[192,192]{1,0:T(8,128)(2,1)} %get-tuple-element.52), channel_id=1, source_target_pairs={{0,4},{4,0},{8,12},{12,8},{16,20},{20,16},{24,28},{28,24},{1,5},{5... | collective-permute-start | bytes 221192 | tf_op jit(solution)/shard_map/ppermute | solution.py:54
  150.0 29.7 %collective-permute-start.30 = (bf16[192,192]{1,0:T(8,128)(2,1)}, bf16[192,192]{1,0:T(8,128)(2,1)}, u32[]{:S(2)}, u32[]{:S(2)}) collective-permute-start(bf16[192,192]{1,0:T(8,128)(2,1)} %get-tuple-element.51), channel_id=1, source_target_pairs={{0,8},{4,12},{8,0},{12,4},{16,24},{20,28},{24,16},{28,20},{1,9},{5... | collective-permute-start | bytes 221192 | tf_op jit(solution)/shard_map/ppermute | solution.py:54
  151.5 30.4 %collective-permute-start.31 = (bf16[192,192]{1,0:T(8,128)(2,1)}, bf16[192,192]{1,0:T(8,128)(2,1)}, u32[]{:S(2)}, u32[]{:S(2)}) collective-permute-start(bf16[192,192]{1,0:T(8,128)(2,1)} %get-tuple-element.50), channel_id=1, source_target_pairs={{0,12},{4,8},{8,4},{12,0},{16,28},{20,24},{24,20},{28,16},{1,13},{... | collective-permute-start | bytes 221192 | tf_op jit(solution)/shard_map/ppermute | solution.py:54
  172.9 38.1 %collective-permute-start.60 = (bf16[2,864,384]{2,1,0:T(8,128)(2,1)}, bf16[2,864,384]{2,1,0:T(8,128)(2,1)S(1)}, u32[]{:S(2)}, u32[]{:S(2)}) collective-permute-start(bf16[2,864,384]{2,1,0:T(8,128)(2,1)} %get-tuple-element.26), channel_id=1, source_target_pairs={{0,4},{4,0},{8,12},{12,8},{16,20},{20,16},{24,28},{28,24},{1,5},{5... | collective-permute-start | bytes 3981320 | tf_op jit(solution)/shard_map/ppermute | solution.py:54
  181.9 19.6 %collective-permute-start.37 = (bf16[192,640]{1,0:T(8,128)(2,1)}, bf16[192,640]{1,0:T(8,128)(2,1)S(1)}, u32[]{:S(2)}, u32[]{:S(2)}) collective-permute-start(bf16[192,640]{1,0:T(8,128)(2,1)} %pad_maximum_fusion.refs_8_), channel_id=1, source_target_pairs={{0,8},{4,12},{8,0},{12,4},{16,24},{20,28},{24,16},{28,20},{1,9},{5... | collective-permute-start | bytes 737288 | tf_op jit(solution)/shard_map/ppermute | solution.py:54
  185.6 17.1 %collective-permute-start.39 = (bf16[192,640]{1,0:T(8,128)(2,1)}, bf16[192,640]{1,0:T(8,128)(2,1)S(1)}, u32[]{:S(2)}, u32[]{:S(2)}) collective-permute-start(bf16[192,640]{1,0:T(8,128)(2,1)} %pad_maximum_fusion.refs_8_), channel_id=1, source_target_pairs={{0,16},{4,20},{8,24},{12,28},{16,0},{20,4},{24,8},{28,12},{1,17},{... | collective-permute-start | bytes 737288 | tf_op jit(solution)/shard_map/ppermute | solution.py:54
  192.8 17.6 %collective-permute-start.61 = (bf16[192,1536]{1,0:T(8,128)(2,1)S(1)}, bf16[192,1536]{1,0:T(8,128)(2,1)S(1)}, u32[]{:S(2)}, u32[]{:S(2)}) collective-permute-start(bf16[192,1536]{1,0:T(8,128)(2,1)S(1)} %copy-done.3), channel_id=1, source_target_pairs={{0,4},{4,0},{8,12},{12,8},{16,20},{20,16},{24,28},{28,24},{1,5},{5... | collective-permute-start | bytes 1769480 | tf_op jit(solution)/shard_map/ppermute | solution.py:54
  207.1 14.4 %collective-permute-start.67 = (bf16[192,384]{1,0:T(8,128)(2,1)S(1)}, bf16[192,384]{1,0:T(8,128)(2,1)}, u32[]{:S(2)}, u32[]{:S(2)}) collective-permute-start(bf16[192,384]{1,0:T(8,128)(2,1)S(1)} %copy-done.42), channel_id=1, source_target_pairs={{0,8},{4,12},{8,0},{12,4},{16,24},{20,28},{24,16},{28,20},{1,9},{5... | collective-permute-start | bytes 442376 | tf_op jit(solution)/shard_map/ppermute | solution.py:54
  222.5 42.3 %collective-permute-start.64 = (bf16[1056,384]{1,0:T(8,128)(2,1)}, bf16[1056,384]{1,0:T(8,128)(2,1)}, u32[]{:S(2)}, u32[]{:S(2)}) collective-permute-start(bf16[1056,384]{1,0:T(8,128)(2,1)} %get-tuple-element.30), channel_id=1, source_target_pairs={{0,8},{4,20},{8,0},{12,28},{16,24},{20,4},{24,16},{28,12},{1,9},{5... | collective-permute-start | bytes 2433032 | tf_op jit(solution)/shard_map/ppermute | solution.py:59
  225.4 13.8 %collective-permute-start.19 = (bf16[48,1536]{1,0:T(8,128)(2,1)S(1)}, bf16[48,1536]{1,0:T(8,128)(2,1)S(1)}, u32[]{:S(2)}, u32[]{:S(2)}) collective-permute-start(bf16[48,1536]{1,0:T(8,128)(2,1)S(1)} %add_convert_fusion.refs_0_), channel_id=1, source_target_pairs={{0,2},{1,3},{2,0},{3,1},{4,6},{5,7},{6,4},{7,5},{8,10},{9,11},{10,... | collective-permute-start | bytes 442376 | tf_op jit(solution)/shard_map/ppermute | solution.py:54
  227.0 14.1 %collective-permute-start.20 = (bf16[48,1536]{1,0:T(8,128)(2,1)S(1)}, bf16[48,1536]{1,0:T(8,128)(2,1)S(1)}, u32[]{:S(2)}, u32[]{:S(2)}) collective-permute-start(bf16[48,1536]{1,0:T(8,128)(2,1)S(1)} %add_convert_fusion.refs_0_), channel_id=1, source_target_pairs={{0,3},{1,2},{2,1},{3,0},{4,7},{5,6},{6,5},{7,4},{8,11},{9,10},{10,... | collective-permute-start | bytes 442376 | tf_op jit(solution)/shard_map/ppermute | solution.py:54
  236.4 16.3 %collective-permute-start.22 = (bf16[48,1536]{1,0:T(8,128)(2,1)S(1)}, bf16[48,1536]{1,0:T(8,128)(2,1)S(1)}, u32[]{:S(2)}, u32[]{:S(2)}) collective-permute-start(bf16[48,1536]{1,0:T(8,128)(2,1)S(1)} %copy-done.44), channel_id=1, source_target_pairs={{0,2},{1,3},{2,0},{3,1},{4,6},{5,7},{6,4},{7,5},{8,10},{9,11},{10,... | collective-permute-start | bytes 442376 | tf_op jit(solution)/shard_map/ppermute | solution.py:54
  241.2 14.6 %collective-permute-start.45 = (f32[48,256]{1,0:T(8,128)S(1)}, f32[48,256]{1,0:T(8,128)S(1)}, u32[]{:S(2)}, u32[]{:S(2)}) collective-permute-start(f32[48,256]{1,0:T(8,128)S(1)} %get-tuple-element.75), channel_id=1, source_target_pairs={{0,3},{1,2},{2,1},{3,0},{4,7},{5,6},{6,5},{7,4},{8,11},{9,10},{10,... | collective-permute-start | bytes 147464 | tf_op jit(solution)/shard_map/ppermute | solution.py:54
  243.7 20.2 %collective-permute-start.44 = (f32[48,256]{1,0:T(8,128)}, f32[48,256]{1,0:T(8,128)S(1)}, u32[]{:S(2)}, u32[]{:S(2)}) collective-permute-start(f32[48,256]{1,0:T(8,128)} %get-tuple-element.76), channel_id=1, source_target_pairs={{0,2},{1,3},{2,0},{3,1},{4,6},{5,7},{6,4},{7,5},{8,10},{9,11},{10,... | collective-permute-start | bytes 147464 | tf_op jit(solution)/shard_map/ppermute | solution.py:54
  254.1 24.3 %collective-permute-start.62 = (bf16[1056,384]{1,0:T(8,128)(2,1)}, bf16[1056,384]{1,0:T(8,128)(2,1)S(1)}, u32[]{:S(2)}, u32[]{:S(2)}) collective-permute-start(bf16[1056,384]{1,0:T(8,128)(2,1)} %get-tuple-element.28), channel_id=1, source_target_pairs={{0,8},{4,12},{8,0},{12,4},{16,24},{20,28},{24,16},{28,20},{1,9},{5... | collective-permute-start | bytes 2433032 | tf_op jit(solution)/shard_map/ppermute | solution.py:54
  256.4 22.5 %collective-permute-start.63 = (bf16[1056,384]{1,0:T(8,128)(2,1)}, bf16[1056,384]{1,0:T(8,128)(2,1)S(1)}, u32[]{:S(2)}, u32[]{:S(2)}) collective-permute-start(bf16[1056,384]{1,0:T(8,128)(2,1)} %get-tuple-element.29), channel_id=1, source_target_pairs={{0,16},{4,20},{8,24},{12,28},{16,0},{20,4},{24,8},{28,12},{1,17},{... | collective-permute-start | bytes 2433032 | tf_op jit(solution)/shard_map/ppermute | solution.py:54
  263.9 27.6 %collective-permute-start.66 = (bf16[192,384]{1,0:T(8,128)(2,1)S(1)}, bf16[192,384]{1,0:T(8,128)(2,1)S(1)}, u32[]{:S(2)}, u32[]{:S(2)}) collective-permute-start(bf16[192,384]{1,0:T(8,128)(2,1)S(1)} %copy-done.42), channel_id=1, source_target_pairs={{0,4},{4,0},{8,12},{12,8},{16,20},{20,16},{24,28},{28,24},{1,5},{5... | collective-permute-start | bytes 442376 | tf_op jit(solution)/shard_map/ppermute | solution.py:54
  264.5 13.8 %collective-permute-start.71 = (bf16[192,384]{1,0:T(8,128)(2,1)}, bf16[192,384]{1,0:T(8,128)(2,1)S(1)}, u32[]{:S(2)}, u32[]{:S(2)}) collective-permute-start(bf16[192,384]{1,0:T(8,128)(2,1)} %broadcast_select_fusion.3), channel_id=1, source_target_pairs={{0,8},{4,20},{8,0},{12,28},{16,24},{20,4},{24,16},{28,12},{1,9},{5... | collective-permute-start | bytes 442376 | tf_op jit(solution)/shard_map/ppermute | solution.py:59
  264.8 19.9 %collective-permute-start.65 = (bf16[1056,384]{1,0:T(8,128)(2,1)}, bf16[1056,384]{1,0:T(8,128)(2,1)}, u32[]{:S(2)}, u32[]{:S(2)}) collective-permute-start(bf16[1056,384]{1,0:T(8,128)(2,1)} %collective-permute-done.64), channel_id=1, source_target_pairs={{0,16},{4,12},{8,24},{12,4},{16,0},{20,28},{24,8},{28,20},{1,17},{... | collective-permute-start | bytes 2433032 | tf_op jit(solution)/shard_map/ppermute | solution.py:59
  (137 other events, 1194.4 us)

commit v2 on v1

--- a/solution.py
+++ b/solution.py
@@ -128,10 +128,9 @@
     tokens, width = normed.shape
     rows = width // parts
     f32, bf16 = jnp.float32, jnp.bfloat16
-    waits = fetch(normed_refs, normed, sems, 0) + fetch(cot_refs, cot, sems, count)
-    for copy in waits:
-        copy.wait()
+    normed_waits, cot_waits = fetch(normed_refs, normed, sems, 0), fetch(cot_refs, cot, sems, count)
     chunk = 256
+    first = tokens // chunk // 2
 
     def forward(step, carry):
         at = pl.ds(pl.multiple_of(step * chunk, chunk), chunk)
@@ -144,7 +143,12 @@
         narrow[:, at] = (gate * sigmoid * up).astype(bf16)
         return carry
 
-    lax.fori_loop(0, tokens // chunk, forward, 0)
+    for copy in normed_waits[: count // 2] + cot_waits[: count // 2]:
+        copy.wait()
+    lax.fori_loop(0, first, forward, 0)
+    for copy in normed_waits[count // 2 :] + cot_waits[count // 2 :]:
+        copy.wait()
+    lax.fori_loop(first, tokens // chunk, forward, 0)
     block = 2 * rows if (2 * rows) % 128 == 0 else width
     per = block // rows
 
@@ -453,7 +457,6 @@
     attn_partial_grad = dot(query_grad, w_query.T) + dot(key_grad, key_own.T) + dot(value_grad, value_own.T)
     d_normed_attn = reduce_tensor(attn_partial_grad)
     factor_blocks = gather_dp(jnp.concatenate([query_grad, key_grad, value_grad], axis=1))
-    grad_gain_attn = jnp.sum(d_normed_attn * input_own * rscale_own, axis=0)
     d_input_own = d_hidden + norm_back(input_own, rscale_own, gain_attn, d_normed_attn)
     d_input_b = lax.optimization_barrier(d_input_own.astype(bf16))
     d_input = arrange(d_input_b, "tensor", tp_rank, f32)
@@ -474,6 +477,7 @@
     summed_key = jnp.concatenate([total[:, :HD] for total in kv_total], axis=1)
     summed_value = jnp.concatenate([total[:, HD:] for total in kv_total], axis=1)
 
+    grad_gain_attn = jnp.sum(attn_partial_grad * input_float * rscale_attn, axis=0)
     bias_query = lax.dynamic_update_slice(
         jnp.zeros((H * HD,), f32),
         jnp.sum(d_query, axis=0).reshape(local_heads * HD),

time: 299 us -> 294 us (0.983)
  waiting for transfers between devices: 57.7 us -> 80.3 us
  other arithmetic: 34.1 us -> 22.9 us
  local copies, waits for them, and re-layouts: 40.2 us -> 29.7 us
  matrix products: 36.4 us -> 32.9 us
    ppermute x67, waiting for transfers between devices: 42 us -> 58 us  [swap(): lax.ppermute(values, axis, [(rank, rank ^ step) for rank in range(size)])]
    ppermute x6, waiting for transfers between devices: 15.8 us -> 22.3 us  [turn(): lax.ppermute(values, 'dp', [(rank, rank ^ steps[rank % 2]) for rank in ra...]
    unnamed x196 -> x252, local copies, waits for them, and re-layouts: 16.1 us -> 11.8 us
    dot_general x13, matrix products: 28.1 us -> 24 us  [dot(): return jnp.dot(a, b, preferred_element_type=f32)]
  transfers between devices with their start and end apart: 73 -> 73, of which waited for: 17 -> 20; matrix products, arithmetic and copies ran while one was open for 34% -> 25% of each run, Pallas kernels for 14% -> 14%
where the time goes in v2:
time: 294 us; the launch traced here: 293 us
  waiting for transfers between devices  80.3 us (27%)
  starting transfers between devices  78.1 us (27%)
  Pallas kernels  46.9 us (16%)
  matrix products  32.9 us (11%)
  local copies, waits for them, and re-layouts  29.7 us (10%)
  other arithmetic  22.9 us (8%)
    ppermute x67, starting transfers between devices, swap(): lax.ppermute(values, axis, [(rank, rank ^ step) for rank in range(size)])  71.3 us
    ppermute x67, waiting for transfers between devices, swap(): lax.ppermute(values, axis, [(rank, rank ^ step) for rank in range(size)])  58 us
    dot_general x13, matrix products, dot(): return jnp.dot(a, b, preferred_element_type=f32)  24 us
    ppermute x6, waiting for transfers between devices, turn(): lax.ppermute(values, 'dp', [(rank, rank ^ steps[rank % 2]) for rank in ra...  22.3 us
    pallas_call x1, Pallas kernels, slice_grads(): pl.pallas_call(functools.partial(slice_kernel, count, parts), out_shape=[...  19.2 us
    unnamed x252, local copies, waits for them, and re-layouts  11.8 us
    pallas_call x4, Pallas kernels, arrange(): pl.pallas_call(arrange_kernel, out_shape=jax.ShapeDtypeStruct((parts * si...  8.5 us
    pallas_call x1, Pallas kernels, place(): pl.pallas_call(functools.partial(place_kernel, padded), out_shape=(wide,...  6.84 us
  transfers between devices with their start and end apart: 73, of which 20 were waited for; matrix products, arithmetic and copies ran while one was open for 25% of the time, Pallas kernels for 14%

profile of v2, /device:TPU:0, one launch (start us, length us, event | category | flops | bytes accessed | tf_op | source)
XLA Modules:
  0.0 293.1 jit_solution(12604670096140485994)
XLA Ops:
  1.2 2.6 collective-permute-start.54
  17.3 3.6 %collective-permute-start.2 = (bf16[48,1536]{1,0:T(8,128)(2,1)}, bf16[48,1536]{1,0:T(8,128)(2,1)S(1)}, u32[]{:S(2)}, u32[]{:S(2)}) collective-permute-start(bf16[48,1536]{1,0:T(8,128)(2,1)} %get-tuple-element.63), channel_id=1, source_target_pairs={{0,3},{1,2},{2,1},{3,0},{4,7},{5,6},{6,5},{7,4},{8,11},{9,10},{10,... | collective-permute-start | bytes 442376 | tf_op jit(solution)/shard_map/ppermute | solution.py:54
  22.8 6.4 %convolution_convert_fusion = bf16[192,2240]{1,0:T(8,128)(2,1)} fusion(bf16[192,1536]{1,0:T(8,128)(2,1)} %refs_8_.1, bf16[2240,1536]{1,0:T(8,128)(2,1)} %param.31), kind=kOutput, calls=%fused_computation | convolution fusion | flops 1321635840 | bytes 8331264 | tf_op jit(solution)/shard_map/dot_general | solution.py:397
  29.2 2.7 dynamic-slice_bitcast_fusion
  36.7 3.0 %collective-permute-start.4 = (bf16[48,1536]{1,0:T(8,128)(2,1)S(1)}, bf16[48,1536]{1,0:T(8,128)(2,1)S(1)}, u32[]{:S(2)}, u32[]{:S(2)}) collective-permute-start(bf16[48,1536]{1,0:T(8,128)(2,1)S(1)} %multiply_convert_fusion.3.refs_0_), channel_id=1, source_target_pairs={{0,2},{1,3},{2,0},{3,1},{4,6},{5,7},{6,4},{7,5},{8,10},{9,11},{10,... | collective-permute-start | bytes 442376 | tf_op jit(solution)/shard_map/ppermute | solution.py:54
  44.0 6.6 %collective-permute-done.4.refs_2_ = bf16[48,1536]{1,0:T(8,128)(2,1)S(1)} collective-permute-done((bf16[48,1536]{1,0:T(8,128)(2,1)S(1)}, bf16[48,1536]{1,0:T(8,128)(2,1)S(1)}, u32[]{:S(2)}, u32[]{:S(2)}) %collective-permute-start.4) | collective-permute-done | bytes 147488 | tf_op jit(solution)/shard_map/ppermute | solution.py:54
  53.4 5.6 %fusion.70 = f32[192,2240]{1,0:T(8,128)S(1)} fusion(bf16[192,1536]{1,0:T(8,128)(2,1)} %arrange.4.refs_0_, bf16[1536,2240]{0,1:T(8,128)(2,1)} %param.30), kind=kOutput, calls=%fused_computation.183 | convolution fusion | flops 1321205760 | bytes 9191424 | tf_op jit(solution)/shard_map/dot_general | solution.py:348
  59.0 5.4 %fusion.69 = f32[192,2240]{1,0:T(8,128)S(1)} fusion(bf16[192,1536]{1,0:T(8,128)(2,1)S(1)} %copy-done.1, bf16[1536,2240]{0,1:T(8,128)(2,1)} %param.29), kind=kOutput, calls=%fused_computation.182 | convolution fusion | flops 1321205760 | bytes 9191424 | tf_op jit(solution)/shard_map/dot_general | solution.py:348
  68.0 2.3 collective-permute-start.11
  76.7 5.3 %collective-permute-done.10 = bf16[48,1536]{1,0:T(8,128)(2,1)S(1)} collective-permute-done((bf16[48,1536]{1,0:T(8,128)(2,1)S(1)}, bf16[48,1536]{1,0:T(8,128)(2,1)S(1)}, u32[]{:S(2)}, u32[]{:S(2)}) %collective-permute-start.10) | collective-permute-done | bytes 147488 | tf_op jit(solution)/shard_map/ppermute | solution.py:54
  84.4 3.1 %collective-permute-start.13 = (bf16[48,1536]{1,0:T(8,128)(2,1)S(1)}, bf16[48,1536]{1,0:T(8,128)(2,1)S(1)}, u32[]{:S(2)}, u32[]{:S(2)}) collective-permute-start(bf16[48,1536]{1,0:T(8,128)(2,1)S(1)} %fusion.61.refs_0_), channel_id=1, source_target_pairs={{0,2},{1,3},{2,0},{3,1},{4,6},{5,7},{6,4},{7,5},{8,10},{9,11},{10,... | collective-permute-start | bytes 442376 | tf_op jit(solution)/shard_map/ppermute | solution.py:54
  92.2 5.9 %collective-permute-done.13.refs_2_ = bf16[48,1536]{1,0:T(8,128)(2,1)S(1)} collective-permute-done((bf16[48,1536]{1,0:T(8,128)(2,1)S(1)}, bf16[48,1536]{1,0:T(8,128)(2,1)S(1)}, u32[]{:S(2)}, u32[]{:S(2)}) %collective-permute-start.13) | collective-permute-done | bytes 147488 | tf_op jit(solution)/shard_map/ppermute | solution.py:54
  113.0 2.4 collective-permute-start.8
  118.1 8.3 %collective-permute-done.49.refs_4_ = bf16[192,1536]{1,0:T(8,128)(2,1)S(1)} collective-permute-done((bf16[192,1536]{1,0:T(8,128)(2,1)S(1)}, bf16[192,1536]{1,0:T(8,128)(2,1)S(1)}, u32[]{:S(2)}, u32[]{:S(2)}) %collective-permute-start.49) | collective-permute-done | bytes 589856 | tf_op jit(solution)/shard_map/ppermute | solution.py:54
  139.2 5.6 %collective-permute-done.51.refs_6_ = bf16[192,1536]{1,0:T(8,128)(2,1)} collective-permute-done((bf16[192,1536]{1,0:T(8,128)(2,1)}, bf16[192,1536]{1,0:T(8,128)(2,1)}, u32[]{:S(2)}, u32[]{:S(2)}) %collective-permute-start.51) | collective-permute-done | bytes 589856 | tf_op jit(solution)/shard_map/ppermute | solution.py:59
  150.2 19.2 %slice_grads.1 = (bf16[2,864,384]{2,1,0:T(8,128)(2,1)}, bf16[2,864,384]{2,1,0:T(8,128)(2,1)}) custom-call(s32[1]{0:T(128)} %bitcast.19.rank, bf16[192,1536]{1,0:T(8,128)(2,1)} %arrange.4.refs_0_, bf16[192,1536]{1,0:T(8,128)(2,1)} %collective-permute-done.46.refs_1_, bf16[192,1536]{1,0:T(8,128)(2,1)} %collective-permute-done.47.refs_2_, ...), custom_call_target="tpu_custom_call" | custom-call | tf_op jit(solution)/shard_map/slice_grads/pallas_call | solution.py:178
  172.6 2.4 collective-permute-start.17
  177.4 7.7 %collective-permute-done.27 = f32[40,128]{1,0:T(8,128)S(1)} collective-permute-done((f32[40,128]{1,0:T(8,128)S(1)}, f32[40,128]{1,0:T(8,128)S(1)}, u32[]{:S(2)}, u32[]{:S(2)}) %collective-permute-start.27) | collective-permute-done | bytes 20512 | tf_op jit(solution)/shard_map/ppermute | solution.py:54
  189.4 3.1 %collective-permute-done.30.refs_2_ = bf16[192,192]{1,0:T(8,128)(2,1)S(1)} collective-permute-done((bf16[192,192]{1,0:T(8,128)(2,1)}, bf16[192,192]{1,0:T(8,128)(2,1)S(1)}, u32[]{:S(2)}, u32[]{:S(2)}) %collective-permute-start.30) | collective-permute-done | bytes 73760 | tf_op jit(solution)/shard_map/ppermute | solution.py:54
  192.6 5.7 %collective-permute-done.31.refs_3_ = bf16[192,192]{1,0:T(8,128)(2,1)S(1)} collective-permute-done((bf16[192,192]{1,0:T(8,128)(2,1)S(1)}, bf16[192,192]{1,0:T(8,128)(2,1)S(1)}, u32[]{:S(2)}, u32[]{:S(2)}) %collective-permute-start.31) | collective-permute-done | bytes 73760 | tf_op jit(solution)/shard_map/ppermute | solution.py:54
  201.6 2.3 collective-permute-done.32.refs_4_
  204.5 3.0 %collective-permute-done.33.refs_5_ = bf16[192,192]{1,0:T(8,128)(2,1)S(1)} collective-permute-done((bf16[192,192]{1,0:T(8,128)(2,1)S(1)}, bf16[192,192]{1,0:T(8,128)(2,1)S(1)}, u32[]{:S(2)}, u32[]{:S(2)}) %collective-permute-start.33) | collective-permute-done | bytes 73760 | tf_op jit(solution)/shard_map/ppermute | solution.py:54
  209.4 2.5 collective-permute-start.28
  215.4 4.4 %pack.1 = (bf16[1056,384]{1,0:T(8,128)(2,1)}, bf16[1056,384]{1,0:T(8,128)(2,1)}, bf16[1056,384]{1,0:T(8,128)(2,1)}, bf16[1056,384]{1,0:T(8,128)(2,1)}) custom-call(s32[1]{0:T(128)} %bitcast.19.rank, bf16[2,864,384]{2,1,0:T(8,128)(2,1)} %get-tuple-element.25.keep, bf16[2,864,384]{2,1,0:T(8,128)(2,1)} %collective-permute-done.60.given, ...), custom_call_target="tpu_custom_call" | custom-call | tf_op jit(solution)/shard_map/pack/pallas_call | solution.py:214
  222.2 2.3 collective-permute-start.19
  227.7 3.4 %outer.2 = f32[192,640]{1,0:T(8,128)} custom-call(bf16[192,192]{1,0:T(8,128)(2,1)} %get-tuple-element.52.refs_0_, bf16[192,192]{1,0:T(8,128)(2,1)} %copy-done.90, bf16[192,192]{1,0:T(8,128)(2,1)} %copy-done.91, bf16[192,192]{1,0:T(8,128)(2,1)} %copy-done.92, bf16[192,192]{1,0:T(8,128)(2,1)} %copy-done.93, bf16[192,192]{1,0:T(8,128)(2,1)} %copy-done.94, ...), custom_call_target="tpu_custom_call" | custom-call | tf_op jit(solution)/shard_map/outer/pallas_call | solution.py:264
  232.8 2.9 collective-permute-start.22
  240.6 8.7 %collective-permute-start.44 = (f32[48,256]{1,0:T(8,128)}, f32[48,256]{1,0:T(8,128)}, u32[]{:S(2)}, u32[]{:S(2)}) collective-permute-start(f32[48,256]{1,0:T(8,128)} %get-tuple-element.75), channel_id=1, source_target_pairs={{0,2},{1,3},{2,0},{3,1},{4,6},{5,7},{6,4},{7,5},{8,10},{9,11},{10,... | collective-permute-start | bytes 147464 | tf_op jit(solution)/shard_map/ppermute | solution.py:54
  262.1 13.4 %collective-permute-done.71.refs_10_ = bf16[192,384]{1,0:T(8,128)(2,1)S(1)} collective-permute-done((bf16[192,384]{1,0:T(8,128)(2,1)S(1)}, bf16[192,384]{1,0:T(8,128)(2,1)S(1)}, u32[]{:S(2)}, u32[]{:S(2)}) %collective-permute-start.71) | collective-permute-done | bytes 147488 | tf_op jit(solution)/shard_map/ppermute | solution.py:59
  277.5 3.4 %collective-permute-done.65.refs_3_ = bf16[1056,384]{1,0:T(8,128)(2,1)} collective-permute-done((bf16[1056,384]{1,0:T(8,128)(2,1)}, bf16[1056,384]{1,0:T(8,128)(2,1)}, u32[]{:S(2)}, u32[]{:S(2)}) %collective-permute-start.65) | collective-permute-done | bytes 811040 | tf_op jit(solution)/shard_map/ppermute | solution.py:59
  280.8 6.8 %place.1 = (f32[192,2240]{1,0:T(8,128)}, f32[192,2240]{1,0:T(8,128)}, f32[192,2240]{1,0:T(8,128)}) custom-call(s32[1]{0:T(128)} %bitcast.19.rank, bf16[1056,384]{1,0:T(8,128)(2,1)} %get-tuple-element.27.refs_0_, bf16[1056,384]{1,0:T(8,128)(2,1)} %copy-done.11, bf16[1056,384]{1,0:T(8,128)(2,1)} %copy-done.12, bf16[1056,384]{1,0:T(8,128)(2,1)} %collective-permute-done.65.refs_3_), custom_call_target="tpu_custom_call" | custom-call | tf_op jit(solution)/shard_map/place/pallas_call | solution.py:243
  288.4 4.5 %outer.3 = f32[192,384]{1,0:T(8,128)} custom-call(bf16[1056,384]{1,0:T(8,128)(2,1)} %get-tuple-element.27.refs_0_, bf16[1056,384]{1,0:T(8,128)(2,1)} %copy-done.11, bf16[1056,384]{1,0:T(8,128)(2,1)} %copy-done.12, bf16[1056,384]{1,0:T(8,128)(2,1)} %collective-permute-done.65.refs_3_, bf16[192,384]{1,0:T(8,128)(2,1)} %copy_bitcast_fusion.2.refs_4_, ...), custom_call_target="tpu_custom_call" | custom-call | tf_op jit(solution)/shard_map/outer/pallas_call | solution.py:294
  (473 shorter events, 126.1 us)
Async XLA Ops:
  0.7 131.0 %collective-permute-start.53 = (bf16[192,1536]{1,0:T(8,128)(2,1)}, bf16[192,1536]{1,0:T(8,128)(2,1)}, u32[]{:S(2)}, u32[]{:S(2)}) collective-permute-start(bf16[192,1536]{1,0:T(8,128)(2,1)} %refs_8_.1), channel_id=1, source_target_pairs={{0,4},{4,0},{8,12},{12,8},{16,20},{20,16},{24,28},{28,24},{1,5},{5... | collective-permute-start | bytes 1769480 | tf_op jit(solution)/shard_map/ppermute | solution.py:54
  1.2 110.2 %collective-permute-start.54 = (bf16[192,1536]{1,0:T(8,128)(2,1)}, bf16[192,1536]{1,0:T(8,128)(2,1)}, u32[]{:S(2)}, u32[]{:S(2)}) collective-permute-start(bf16[192,1536]{1,0:T(8,128)(2,1)} %refs_8_.1), channel_id=1, source_target_pairs={{0,8},{4,12},{8,0},{12,4},{16,24},{20,28},{24,16},{28,20},{1,9},{5... | collective-permute-start | bytes 1769480 | tf_op jit(solution)/shard_map/ppermute | solution.py:54
  17.3 14.7 %collective-permute-start.2 = (bf16[48,1536]{1,0:T(8,128)(2,1)}, bf16[48,1536]{1,0:T(8,128)(2,1)S(1)}, u32[]{:S(2)}, u32[]{:S(2)}) collective-permute-start(bf16[48,1536]{1,0:T(8,128)(2,1)} %get-tuple-element.63), channel_id=1, source_target_pairs={{0,3},{1,2},{2,1},{3,0},{4,7},{5,6},{6,5},{7,4},{8,11},{9,10},{10,... | collective-permute-start | bytes 442376 | tf_op jit(solution)/shard_map/ppermute | solution.py:54
  20.9 13.0 %collective-permute-start.1 = (bf16[48,1536]{1,0:T(8,128)(2,1)}, bf16[48,1536]{1,0:T(8,128)(2,1)S(1)}, u32[]{:S(2)}, u32[]{:S(2)}) collective-permute-start(bf16[48,1536]{1,0:T(8,128)(2,1)} %get-tuple-element.64), channel_id=1, source_target_pairs={{0,2},{1,3},{2,0},{3,1},{4,6},{5,7},{6,4},{7,5},{8,10},{9,11},{10,... | collective-permute-start | bytes 442376 | tf_op jit(solution)/shard_map/ppermute | solution.py:54
  20.9 13.0 %collective-permute-start = (bf16[48,1536]{1,0:T(8,128)(2,1)}, bf16[48,1536]{1,0:T(8,128)(2,1)}, u32[]{:S(2)}, u32[]{:S(2)}) collective-permute-start(bf16[48,1536]{1,0:T(8,128)(2,1)} %get-tuple-element.62), channel_id=1, source_target_pairs={{0,1},{1,0},{2,3},{3,2},{4,5},{5,4},{6,7},{7,6},{8,9},{9,8},{10,11... | collective-permute-start | bytes 442376 | tf_op jit(solution)/shard_map/ppermute | solution.py:54
  36.7 13.9 %collective-permute-start.4 = (bf16[48,1536]{1,0:T(8,128)(2,1)S(1)}, bf16[48,1536]{1,0:T(8,128)(2,1)S(1)}, u32[]{:S(2)}, u32[]{:S(2)}) collective-permute-start(bf16[48,1536]{1,0:T(8,128)(2,1)S(1)} %multiply_convert_fusion.3.refs_0_), channel_id=1, source_target_pairs={{0,2},{1,3},{2,0},{3,1},{4,6},{5,7},{6,4},{7,5},{8,10},{9,11},{10,... | collective-permute-start | bytes 442376 | tf_op jit(solution)/shard_map/ppermute | solution.py:54
  84.4 13.8 %collective-permute-start.13 = (bf16[48,1536]{1,0:T(8,128)(2,1)S(1)}, bf16[48,1536]{1,0:T(8,128)(2,1)S(1)}, u32[]{:S(2)}, u32[]{:S(2)}) collective-permute-start(bf16[48,1536]{1,0:T(8,128)(2,1)S(1)} %fusion.61.refs_0_), channel_id=1, source_target_pairs={{0,2},{1,3},{2,0},{3,1},{4,6},{5,7},{6,4},{7,5},{8,10},{9,11},{10,... | collective-permute-start | bytes 442376 | tf_op jit(solution)/shard_map/ppermute | solution.py:54
  90.7 22.3 %collective-permute-start.56 = (bf16[192,1536]{1,0:T(8,128)(2,1)}, bf16[192,1536]{1,0:T(8,128)(2,1)}, u32[]{:S(2)}, u32[]{:S(2)}) collective-permute-start(bf16[192,1536]{1,0:T(8,128)(2,1)} %refs_8_.1), channel_id=1, source_target_pairs={{0,16},{4,20},{8,24},{12,28},{16,0},{20,4},{24,8},{28,12},{1,17},{... | collective-permute-start | bytes 1769480 | tf_op jit(solution)/shard_map/ppermute | solution.py:54
  98.2 40.2 %collective-permute-start.46 = (bf16[192,1536]{1,0:T(8,128)(2,1)S(1)}, bf16[192,1536]{1,0:T(8,128)(2,1)}, u32[]{:S(2)}, u32[]{:S(2)}) collective-permute-start(bf16[192,1536]{1,0:T(8,128)(2,1)S(1)} %copy-done.1), channel_id=1, source_target_pairs={{0,4},{4,0},{8,12},{12,8},{16,20},{20,16},{24,28},{28,24},{1,5},{5... | collective-permute-start | bytes 1769480 | tf_op jit(solution)/shard_map/ppermute | solution.py:54
  99.5 17.9 %collective-permute-start.47 = (bf16[192,1536]{1,0:T(8,128)(2,1)S(1)}, bf16[192,1536]{1,0:T(8,128)(2,1)}, u32[]{:S(2)}, u32[]{:S(2)}) collective-permute-start(bf16[192,1536]{1,0:T(8,128)(2,1)S(1)} %copy-done.1), channel_id=1, source_target_pairs={{0,8},{4,12},{8,0},{12,4},{16,24},{20,28},{24,16},{28,20},{1,9},{5... | collective-permute-start | bytes 1769480 | tf_op jit(solution)/shard_map/ppermute | solution.py:54
  111.5 14.9 %collective-permute-start.49 = (bf16[192,1536]{1,0:T(8,128)(2,1)S(1)}, bf16[192,1536]{1,0:T(8,128)(2,1)S(1)}, u32[]{:S(2)}, u32[]{:S(2)}) collective-permute-start(bf16[192,1536]{1,0:T(8,128)(2,1)S(1)} %copy-done.1), channel_id=1, source_target_pairs={{0,16},{4,20},{8,24},{12,28},{16,0},{20,4},{24,8},{28,12},{1,17},{... | collective-permute-start | bytes 1769480 | tf_op jit(solution)/shard_map/ppermute | solution.py:54
  113.0 15.0 %collective-permute-start.8 = (bf16[48,1536]{1,0:T(8,128)(2,1)}, bf16[48,1536]{1,0:T(8,128)(2,1)S(1)}, u32[]{:S(2)}, u32[]{:S(2)}) collective-permute-start(bf16[48,1536]{1,0:T(8,128)(2,1)} %get-tuple-element.60), channel_id=1, source_target_pairs={{0,3},{1,2},{2,1},{3,0},{4,7},{5,6},{6,5},{7,4},{8,11},{9,10},{10,... | collective-permute-start | bytes 442376 | tf_op jit(solution)/shard_map/ppermute | solution.py:54
  131.7 13.1 %collective-permute-start.51 = (bf16[192,1536]{1,0:T(8,128)(2,1)}, bf16[192,1536]{1,0:T(8,128)(2,1)}, u32[]{:S(2)}, u32[]{:S(2)}) collective-permute-start(bf16[192,1536]{1,0:T(8,128)(2,1)} %broadcast_select_fusion.1), channel_id=1, source_target_pairs={{0,8},{4,20},{8,0},{12,28},{16,24},{20,4},{24,16},{28,12},{1,9},{5... | collective-permute-start | bytes 1769480 | tf_op jit(solution)/shard_map/ppermute | solution.py:59
  144.8 25.0 %collective-permute-start.25 = (f32[40,128]{1,0:T(8,128)S(1)}, f32[40,128]{1,0:T(8,128)S(1)}, u32[]{:S(2)}, u32[]{:S(2)}) collective-permute-start(f32[40,128]{1,0:T(8,128)S(1)} %bitcast_add_fusion), channel_id=1, source_target_pairs={{0,8},{4,12},{8,0},{12,4},{16,24},{20,28},{24,16},{28,20},{1,9},{5... | collective-permute-start | bytes 61448 | tf_op jit(solution)/shard_map/ppermute | solution.py:54
  169.5 42.4 %collective-permute-start.60 = (bf16[2,864,384]{2,1,0:T(8,128)(2,1)}, bf16[2,864,384]{2,1,0:T(8,128)(2,1)}, u32[]{:S(2)}, u32[]{:S(2)}) collective-permute-start(bf16[2,864,384]{2,1,0:T(8,128)(2,1)} %get-tuple-element.26), channel_id=1, source_target_pairs={{0,4},{4,0},{8,12},{12,8},{16,20},{20,16},{24,28},{28,24},{1,5},{5... | collective-permute-start | bytes 3981320 | tf_op jit(solution)/shard_map/ppermute | solution.py:54
  172.6 14.7 %collective-permute-start.17 = (bf16[48,1536]{1,0:T(8,128)(2,1)S(1)}, bf16[48,1536]{1,0:T(8,128)(2,1)S(1)}, u32[]{:S(2)}, u32[]{:S(2)}) collective-permute-start(bf16[48,1536]{1,0:T(8,128)(2,1)S(1)} %get-tuple-element.54), channel_id=1, source_target_pairs={{0,3},{1,2},{2,1},{3,0},{4,7},{5,6},{6,5},{7,4},{8,11},{9,10},{10,... | collective-permute-start | bytes 442376 | tf_op jit(solution)/shard_map/ppermute | solution.py:54
  175.0 13.7 %collective-permute-start.16 = (bf16[48,1536]{1,0:T(8,128)(2,1)S(1)}, bf16[48,1536]{1,0:T(8,128)(2,1)S(1)}, u32[]{:S(2)}, u32[]{:S(2)}) collective-permute-start(bf16[48,1536]{1,0:T(8,128)(2,1)S(1)} %get-tuple-element.55), channel_id=1, source_target_pairs={{0,2},{1,3},{2,0},{3,1},{4,6},{5,7},{6,4},{7,5},{8,10},{9,11},{10,... | collective-permute-start | bytes 442376 | tf_op jit(solution)/shard_map/ppermute | solution.py:54
  175.3 13.9 %collective-permute-start.15 = (bf16[48,1536]{1,0:T(8,128)(2,1)S(1)}, bf16[48,1536]{1,0:T(8,128)(2,1)S(1)}, u32[]{:S(2)}, u32[]{:S(2)}) collective-permute-start(bf16[48,1536]{1,0:T(8,128)(2,1)S(1)} %get-tuple-element.53), channel_id=1, source_target_pairs={{0,1},{1,0},{2,3},{3,2},{4,5},{5,4},{6,7},{7,6},{8,9},{9,8},{10,11... | collective-permute-start | bytes 442376 | tf_op jit(solution)/shard_map/ppermute | solution.py:54
  189.2 20.2 %collective-permute-start.61 = (bf16[192,1536]{1,0:T(8,128)(2,1)S(1)}, bf16[192,1536]{1,0:T(8,128)(2,1)S(1)}, u32[]{:S(2)}, u32[]{:S(2)}) collective-permute-start(bf16[192,1536]{1,0:T(8,128)(2,1)S(1)} %copy-done.4), channel_id=1, source_target_pairs={{0,4},{4,0},{8,12},{12,8},{16,20},{20,16},{24,28},{28,24},{1,5},{5... | collective-permute-start | bytes 1769480 | tf_op jit(solution)/shard_map/ppermute | solution.py:54
  204.0 15.9 %collective-permute-start.67 = (bf16[192,384]{1,0:T(8,128)(2,1)}, bf16[192,384]{1,0:T(8,128)(2,1)}, u32[]{:S(2)}, u32[]{:S(2)}) collective-permute-start(bf16[192,384]{1,0:T(8,128)(2,1)} %copy_bitcast_fusion.2.refs_4_), channel_id=1, source_target_pairs={{0,8},{4,12},{8,0},{12,4},{16,24},{20,28},{24,16},{28,20},{1,9},{5... | collective-permute-start | bytes 442376 | tf_op jit(solution)/shard_map/ppermute | solution.py:54
  220.9 39.3 %collective-permute-start.64 = (bf16[1056,384]{1,0:T(8,128)(2,1)}, bf16[1056,384]{1,0:T(8,128)(2,1)}, u32[]{:S(2)}, u32[]{:S(2)}) collective-permute-start(bf16[1056,384]{1,0:T(8,128)(2,1)} %get-tuple-element.30), channel_id=1, source_target_pairs={{0,8},{4,20},{8,0},{12,28},{16,24},{20,4},{24,16},{28,12},{1,9},{5... | collective-permute-start | bytes 2433032 | tf_op jit(solution)/shard_map/ppermute | solution.py:59
  222.2 14.0 %collective-permute-start.19 = (bf16[48,1536]{1,0:T(8,128)(2,1)S(1)}, bf16[48,1536]{1,0:T(8,128)(2,1)S(1)}, u32[]{:S(2)}, u32[]{:S(2)}) collective-permute-start(bf16[48,1536]{1,0:T(8,128)(2,1)S(1)} %add_convert_fusion.refs_0_), channel_id=1, source_target_pairs={{0,2},{1,3},{2,0},{3,1},{4,6},{5,7},{6,4},{7,5},{8,10},{9,11},{10,... | collective-permute-start | bytes 442376 | tf_op jit(solution)/shard_map/ppermute | solution.py:54
  224.5 13.6 %collective-permute-start.20 = (bf16[48,1536]{1,0:T(8,128)(2,1)S(1)}, bf16[48,1536]{1,0:T(8,128)(2,1)S(1)}, u32[]{:S(2)}, u32[]{:S(2)}) collective-permute-start(bf16[48,1536]{1,0:T(8,128)(2,1)S(1)} %add_convert_fusion.refs_0_), channel_id=1, source_target_pairs={{0,3},{1,2},{2,1},{3,0},{4,7},{5,6},{6,5},{7,4},{8,11},{9,10},{10,... | collective-permute-start | bytes 442376 | tf_op jit(solution)/shard_map/ppermute | solution.py:54
  232.8 17.1 %collective-permute-start.22 = (bf16[48,1536]{1,0:T(8,128)(2,1)S(1)}, bf16[48,1536]{1,0:T(8,128)(2,1)S(1)}, u32[]{:S(2)}, u32[]{:S(2)}) collective-permute-start(bf16[48,1536]{1,0:T(8,128)(2,1)S(1)} %copy-done.49), channel_id=1, source_target_pairs={{0,2},{1,3},{2,0},{3,1},{4,6},{5,7},{6,4},{7,5},{8,10},{9,11},{10,... | collective-permute-start | bytes 442376 | tf_op jit(solution)/shard_map/ppermute | solution.py:54
  236.2 13.7 %collective-permute-start.23 = (bf16[48,1536]{1,0:T(8,128)(2,1)S(1)}, bf16[48,1536]{1,0:T(8,128)(2,1)S(1)}, u32[]{:S(2)}, u32[]{:S(2)}) collective-permute-start(bf16[48,1536]{1,0:T(8,128)(2,1)S(1)} %copy-done.49), channel_id=1, source_target_pairs={{0,3},{1,2},{2,1},{3,0},{4,7},{5,6},{6,5},{7,4},{8,11},{9,10},{10,... | collective-permute-start | bytes 442376 | tf_op jit(solution)/shard_map/ppermute | solution.py:54
  238.1 14.8 %collective-permute-start.45 = (f32[48,256]{1,0:T(8,128)S(1)}, f32[48,256]{1,0:T(8,128)S(1)}, u32[]{:S(2)}, u32[]{:S(2)}) collective-permute-start(f32[48,256]{1,0:T(8,128)S(1)} %get-tuple-element.74), channel_id=1, source_target_pairs={{0,3},{1,2},{2,1},{3,0},{4,7},{5,6},{6,5},{7,4},{8,11},{9,10},{10,... | collective-permute-start | bytes 147464 | tf_op jit(solution)/shard_map/ppermute | solution.py:54
  240.6 18.9 %collective-permute-start.44 = (f32[48,256]{1,0:T(8,128)}, f32[48,256]{1,0:T(8,128)}, u32[]{:S(2)}, u32[]{:S(2)}) collective-permute-start(f32[48,256]{1,0:T(8,128)} %get-tuple-element.75), channel_id=1, source_target_pairs={{0,2},{1,3},{2,0},{3,1},{4,6},{5,7},{6,4},{7,5},{8,10},{9,11},{10,... | collective-permute-start | bytes 147464 | tf_op jit(solution)/shard_map/ppermute | solution.py:54
  251.2 24.3 %collective-permute-start.62 = (bf16[1056,384]{1,0:T(8,128)(2,1)}, bf16[1056,384]{1,0:T(8,128)(2,1)S(1)}, u32[]{:S(2)}, u32[]{:S(2)}) collective-permute-start(bf16[1056,384]{1,0:T(8,128)(2,1)} %get-tuple-element.28), channel_id=1, source_target_pairs={{0,8},{4,12},{8,0},{12,4},{16,24},{20,28},{24,16},{28,20},{1,9},{5... | collective-permute-start | bytes 2433032 | tf_op jit(solution)/shard_map/ppermute | solution.py:54
  252.9 23.2 %collective-permute-start.63 = (bf16[1056,384]{1,0:T(8,128)(2,1)}, bf16[1056,384]{1,0:T(8,128)(2,1)S(1)}, u32[]{:S(2)}, u32[]{:S(2)}) collective-permute-start(bf16[1056,384]{1,0:T(8,128)(2,1)} %get-tuple-element.29), channel_id=1, source_target_pairs={{0,16},{4,20},{8,24},{12,28},{16,0},{20,4},{24,8},{28,12},{1,17},{... | collective-permute-start | bytes 2433032 | tf_op jit(solution)/shard_map/ppermute | solution.py:54
  259.6 28.1 %collective-permute-start.66 = (bf16[192,384]{1,0:T(8,128)(2,1)}, bf16[192,384]{1,0:T(8,128)(2,1)S(1)}, u32[]{:S(2)}, u32[]{:S(2)}) collective-permute-start(bf16[192,384]{1,0:T(8,128)(2,1)} %copy_bitcast_fusion.2.refs_4_), channel_id=1, source_target_pairs={{0,4},{4,0},{8,12},{12,8},{16,20},{20,16},{24,28},{28,24},{1,5},{5... | collective-permute-start | bytes 442376 | tf_op jit(solution)/shard_map/ppermute | solution.py:54
  259.6 15.9 %collective-permute-start.71 = (bf16[192,384]{1,0:T(8,128)(2,1)S(1)}, bf16[192,384]{1,0:T(8,128)(2,1)S(1)}, u32[]{:S(2)}, u32[]{:S(2)}) collective-permute-start(bf16[192,384]{1,0:T(8,128)(2,1)S(1)} %broadcast_select_fusion.3), channel_id=1, source_target_pairs={{0,8},{4,20},{8,0},{12,28},{16,24},{20,4},{24,16},{28,12},{1,9},{5... | collective-permute-start | bytes 442376 | tf_op jit(solution)/shard_map/ppermute | solution.py:59
  260.2 20.6 %collective-permute-start.65 = (bf16[1056,384]{1,0:T(8,128)(2,1)}, bf16[1056,384]{1,0:T(8,128)(2,1)}, u32[]{:S(2)}, u32[]{:S(2)}) collective-permute-start(bf16[1056,384]{1,0:T(8,128)(2,1)} %collective-permute-done.64), channel_id=1, source_target_pairs={{0,16},{4,12},{8,24},{12,4},{16,0},{20,28},{24,8},{28,20},{1,17},{... | collective-permute-start | bytes 2433032 | tf_op jit(solution)/shard_map/ppermute | solution.py:59
  (165 other events, 1470.8 us)
